TPU v7x, 32 devices: a whole 2x2x4 slice. The times are simulated.
32 devices in a mesh: fsdp: 4 (over z), ctx: 4 (over x, core), tp: 2 (over y).
Axes of the slice: x: 2, y: 2, z: 4, core: 2. Of those that a mesh axis runs over, the one named last changes fastest.
Arguments:
- tokens: bfloat16 [4, 1536, 2048], P('fsdp', 'ctx'), may hold values from -6 to 6
- seq_ids: int32 [4, 1536], P('fsdp'), may hold values from 0 to 2, never falling along the last dimension, each value on 1 to 768 neighbouring positions
- pic_starts: int32 [4, 3], P('fsdp'), may hold values from 0 to 1408, as said below
- pic_lengths: int32 [4, 3], P('fsdp'), may hold values from 128 to 256, as said below
- skip_mask: int32 [4, 1536], P('fsdp', 'ctx'), may hold values 0 or 1
- w_query: bfloat16 [2048, 2048], P('fsdp', 'tp'), may hold values from -0.125 to 0.125
- w_key: bfloat16 [2048, 512], P('fsdp', 'tp'), may hold values from -0.125 to 0.125
- w_value: bfloat16 [2048, 512], P('fsdp', 'tp'), may hold values from -0.125 to 0.125
- w_out: bfloat16 [2048, 2048], P('tp', 'fsdp'), may hold values from -1 to 1
- w_gate: bfloat16 [2048, 5632], P('fsdp', 'tp'), may hold values from -0.125 to 0.125
- w_up: bfloat16 [2048, 5632], P('fsdp', 'tp'), may hold values from -0.125 to 0.125
- w_down: bfloat16 [5632, 2048], P('tp', 'fsdp'), may hold values from -0.078125 to 0.078125
- gain_attn: bfloat16 [2048], P('fsdp'), may hold values from 0.25 to 1.75
- gain_ffn: bfloat16 [2048], P('fsdp'), may hold values from 0.25 to 1.75
- cotangent: bfloat16 [4, 1536, 2048], P('fsdp', 'ctx'), may hold values from -6 to 6
Outputs:
- output: bfloat16 [4, 1536, 2048], P('fsdp', 'ctx')
- input_grad: bfloat16 [4, 1536, 2048], P('fsdp', 'ctx')
- grad_query: float32 [2048, 2048], P('fsdp', 'tp')
- grad_key: float32 [2048, 512], P('fsdp', 'tp')
- grad_value: float32 [2048, 512], P('fsdp', 'tp')
- grad_out: float32 [2048, 2048], P('tp', 'fsdp')
- grad_gate: float32 [2048, 5632], P('fsdp', 'tp')
- grad_up: float32 [2048, 5632], P('fsdp', 'tp')
- grad_down: float32 [5632, 2048], P('tp', 'fsdp')
- grad_gain_attn: float32 [2048], P('fsdp')
- grad_gain_ffn: float32 [2048], P('fsdp')
Inputs may be any that keep to these rules, and one draw needn't show every extreme that they name: `pic_starts`: picture p of a row (counting from 0) lies inside positions p * 2 * 256 to (p + 1) * 2 * 256 - 1, so pictures never intersect; it may start anywhere in that range where it fits. `pic_lengths`: every row has a picture of exactly 256 positions and another of exactly 128.
All inputs are finite; a program needn't handle non-finite values. No bound on the sum of `skip_mask` on one device may be relied on, other than what follows from the above.
Results may differ from a plain program's by a relative error of at most 0.022.
Values may be sent and summed in bfloat16 or wider, within the bound.
No kernel may reach another device: no remote copies, remote signals or barrier semaphores. Data moves between devices by JAX's collectives and lax.ppermute only.
A program may use at most 256 MiB of HBM per device.

v0:
```python
import math
import jax
import jax.numpy as jnp
from jax import lax
from jax.sharding import PartitionSpec as P

HEAD = 128
norm_eps = 1e-05
rope_base = 10000.0
F32 = jnp.float32
BF16 = jnp.bfloat16


def dot(a, b, ca, cb):
    return lax.dot_general(a, b, (((ca,), (cb,)), ((), ())), preferred_element_type=F32)


def rope_tables(positions):
    half_width = HEAD // 2
    frequency = jnp.power(rope_base, -jnp.arange(half_width, dtype=F32) * 2.0 / HEAD)
    angles = positions.astype(F32)[:, None] * frequency[None, :]
    return (jnp.cos(angles), jnp.sin(angles))


def rotate(u, cosine, sine):
    half_width = HEAD // 2
    parts = []
    for head in range(u.shape[1] // HEAD):
        first = u[:, head * HEAD : head * HEAD + half_width]
        second = u[:, head * HEAD + half_width : (head + 1) * HEAD]
        parts += [first * cosine - second * sine, second * cosine + first * sine]
    return jnp.concatenate(parts, axis=1)


def picture_ids(starts, lengths, positions):
    inside = (positions[:, None] >= starts[None, :]) & (
        positions[:, None] < starts[None, :] + lengths[None, :]
    )
    numbers = jnp.arange(1, starts.shape[0] + 1, dtype=jnp.int32)
    return jnp.sum(jnp.where(inside, numbers[None, :], 0), axis=1)


def allowed_mask(query_pos, key_pos, query_doc, key_doc, query_pic, key_pic):
    same_doc = query_doc[:, None] == key_doc[None, :]
    causal = key_pos[None, :] <= query_pos[:, None]
    picture = (query_pic[:, None] == key_pic[None, :]) & (query_pic[:, None] > 0)
    return same_doc & (causal | picture)


def norm_back(d_normed, hat, inv_rms, gain):
    scaled = d_normed * gain
    return inv_rms * (scaled - hat * jnp.mean(scaled * hat, axis=-1, keepdims=True))


def far(v):
    return lax.ppermute(v, "ctx", [(i, i ^ 2) for i in range(4)])


def near(v):
    return lax.ppermute(v, "ctx", [(i, i ^ 1) for i in range(4)])


def side(v):
    return lax.ppermute(v, "tp", [(0, 1), (1, 0)])


def spread(v):
    n, w = v.shape
    left, right = (v[:, : w // 2], v[:, w // 2 :])
    left_far = far(left)
    right_side = side(right)
    left_two = side(jnp.concatenate([left, left_far], axis=0))
    right_two = far(jnp.concatenate([right, right_side], axis=0))
    left_all = jnp.concatenate([left, left_two[:n], left_far, left_two[n:]], axis=0)
    right_all = jnp.concatenate([right, right_side, right_two], axis=0)
    mine = jnp.concatenate([left_all, right_all], axis=1)
    return jnp.concatenate([mine, near(mine)], axis=0)


def collect(p):
    n, w = (p.shape[0] // 8, p.shape[1])
    both = p[: 4 * n].astype(F32) + near(p[4 * n :]).astype(F32)
    both = both.astype(BF16)
    left, right = (both[:, : w // 2], both[:, w // 2 :].reshape(2, 2, n, w // 2))
    left_far = far(left[2 * n :])
    right_side = side(right[:, 1].reshape(2 * n, w // 2))
    left = (left[: 2 * n].astype(F32) + left_far.astype(F32)).astype(BF16)
    right = (right[:, 0].reshape(2 * n, w // 2).astype(F32) + right_side.astype(F32)).astype(BF16)
    left_side = side(left[n:])
    right_far = far(right[n:])
    return jnp.concatenate(
        [
            left[:n].astype(F32) + left_side.astype(F32),
            right[:n].astype(F32) + right_far.astype(F32),
        ],
        axis=1,
    )


def both_sides(v, t):
    other = side(v)
    return jnp.where(
        t == 0, jnp.concatenate([v, other], axis=0), jnp.concatenate([other, v], axis=0)
    )


def ctx_rows(v, c):
    n = v.shape[0]
    two = jnp.stack([v, far(v)])
    other = near(two)
    out = jnp.zeros((4, n, v.shape[1]), v.dtype)
    for bits, piece in ((0, two[0]), (2, two[1]), (1, other[0]), (3, other[1])):
        out = lax.dynamic_update_slice(out, piece[None], (c ^ bits, 0, 0))
    return out


def swap_halves(v):
    n = v.shape[0] // 2
    return jnp.concatenate([v[n:], v[:n]], axis=0)


def body(
    tokens,
    seq_ids,
    pic_starts,
    pic_lengths,
    skip_mask,
    w_query,
    w_key,
    w_value,
    w_out,
    w_gate,
    w_up,
    w_down,
    gain_attn,
    gain_ffn,
    cotangent,
):
    tok_rows = tokens.shape[1]
    width = tokens.shape[2]
    own = tok_rows // 2
    seq_len = seq_ids.shape[1]
    c = lax.axis_index("ctx")
    t = lax.axis_index("tp")
    core = c & 1
    q_cols = w_query.shape[1] // 4
    heads = q_cols // HEAD
    ff = w_gate.shape[1] // 4
    query_scale = 1.0 / math.sqrt(HEAD)
    wq_t = lax.dynamic_slice_in_dim(w_query, c * q_cols, q_cols, 1).T
    w_kv = jnp.where(core == 0, w_key, w_value)
    wkv_t = lax.dynamic_slice_in_dim(w_kv, (c >> 1) * HEAD, HEAD, 1).T
    gains = jnp.concatenate(
        [gain_attn[None], gain_ffn[None], jnp.zeros((14, gain_attn.shape[0]), BF16)], axis=0
    )
    first = lax.all_gather(
        jnp.concatenate([wq_t, wkv_t, gains], axis=0), "fsdp", axis=1, tiled=True
    )
    qkv_cols = q_cols + HEAD
    wqkv = first[:qkv_cols]
    gain_one = first[qkv_cols].astype(F32)
    gain_two = first[qkv_cols + 1].astype(F32)
    wo = lax.all_gather(
        lax.dynamic_slice_in_dim(w_out, c * q_cols, q_cols, 0), "fsdp", axis=1, tiled=True
    )
    wg_t = lax.dynamic_slice_in_dim(w_gate, c * ff, ff, 1).T
    wu_t = lax.dynamic_slice_in_dim(w_up, c * ff, ff, 1).T
    wgu = lax.all_gather(jnp.concatenate([wg_t, wu_t], axis=0), "fsdp", axis=1, tiled=True)
    wd = lax.all_gather(lax.dynamic_slice_in_dim(w_down, c * ff, ff, 0), "fsdp", axis=1, tiled=True)
    x_own_b = lax.dynamic_slice_in_dim(tokens[0], t * own, own, 0)
    x_own = x_own_b.astype(F32)
    keep_own = lax.dynamic_slice_in_dim(skip_mask[0], t * own, own, 0).astype(F32)[:, None]
    dy_own = lax.dynamic_slice_in_dim(cotangent[0], t * own, own, 0).astype(F32)
    d_ffn_own = (keep_own * dy_own).astype(BF16)
    pos_list = []
    for block in range(8):
        near_bit, far_bit, side_bit = (block >> 2, block >> 1 & 1, block & 1)
        start = (c ^ near_bit + 2 * far_bit) * tok_rows + (t ^ side_bit) * own
        pos_list.append(start)
    positions = jnp.concatenate([s + jnp.arange(own, dtype=jnp.int32) for s in pos_list])
    docs = jnp.concatenate([lax.dynamic_slice_in_dim(seq_ids[0], s, own, 0) for s in pos_list])
    pics = picture_ids(pic_starts[0], pic_lengths[0], positions)
    allowed = allowed_mask(positions, positions, docs, docs, pics, pics)
    cosine, sine = rope_tables(positions)
    x_all = spread(x_own_b).astype(F32)
    inv_all = lax.rsqrt(jnp.mean(x_all * x_all, axis=-1, keepdims=True) + norm_eps)
    n1 = (x_all * inv_all * gain_one).astype(BF16)
    qkv_pre = dot(n1, wqkv, 1, 1)
    queries = (rotate(qkv_pre[:, :q_cols], cosine, sine) * query_scale).astype(BF16)
    kv_pre = qkv_pre[:, q_cols:]
    kv_own = jnp.where(core == 0, rotate(kv_pre, cosine, sine), kv_pre).astype(BF16)
    kv_other = swap_halves(near(kv_own))
    keys = jnp.where(core == 0, kv_own, kv_other)
    values = jnp.where(core == 0, kv_other, kv_own)
    q_heads = queries.reshape(seq_len, heads, HEAD)
    scores = jnp.einsum("qhd,kd->hqk", q_heads, keys, preferred_element_type=F32)
    masked = jnp.where(allowed[None], scores, -1e30)
    row_max = jnp.max(masked, axis=-1, keepdims=True)
    exp_scores = jnp.exp(masked - row_max)
    row_total = jnp.sum(exp_scores, axis=-1, keepdims=True)
    soft_b = (exp_scores / row_total).astype(BF16)
    log_total = row_max + jnp.log(row_total)
    head_out = (
        jnp.einsum("hqk,kd->qhd", soft_b, values, preferred_element_type=F32)
        .reshape(seq_len, q_cols)
        .astype(BF16)
    )
    attn = collect(dot(head_out, wo, 1, 0).astype(BF16))
    mid = x_own + keep_own * attn
    inv_two = lax.rsqrt(jnp.mean(mid * mid, axis=-1, keepdims=True) + norm_eps)
    hat_two = mid * inv_two
    n2 = spread((hat_two * gain_two).astype(BF16))
    d_ffn = spread(d_ffn_own)
    gu = dot(wgu, n2, 1, 1)
    gate, up = (gu[:ff], gu[ff:])
    sig = jax.nn.sigmoid(gate)
    hidden = (gate * sig * up).astype(BF16)
    d_hidden = dot(wd, d_ffn, 1, 1)
    d_gate = (d_hidden * up * sig * (1.0 + gate * (1.0 - sig))).astype(BF16)
    d_up = (d_hidden * (gate * sig)).astype(BF16)
    d_gu = jnp.concatenate([d_gate, d_up], axis=0)
    d_n2 = collect(dot(d_gu, wgu, 0, 0).astype(BF16))
    grad_gu = dot(d_gu, n2, 1, 0).astype(BF16)
    grad_down = dot(hidden, d_ffn, 1, 0).astype(BF16)
    shard_gu = lax.psum_scatter(grad_gu, "fsdp", scatter_dimension=1, tiled=True)
    shard_down = lax.psum_scatter(grad_down, "fsdp", scatter_dimension=1, tiled=True)
    ffn = collect(dot(hidden, wd, 0, 0).astype(BF16))
    output = both_sides((mid + keep_own * ffn).astype(BF16), t)
    d_mid = dy_own + norm_back(d_n2, hat_two, inv_two, gain_two)
    d_attn = spread((keep_own * d_mid).astype(BF16))
    grad_out = dot(head_out, d_attn, 0, 0).astype(BF16)
    shard_out = lax.psum_scatter(grad_out, "fsdp", scatter_dimension=1, tiled=True)
    d_head = dot(d_attn, wo, 1, 1).astype(BF16).reshape(seq_len, heads, HEAD)
    scores = jnp.einsum("qhd,kd->hqk", q_heads, keys, preferred_element_type=F32)
    soft = jnp.where(allowed[None], jnp.exp(scores - log_total), 0.0)
    d_soft = jnp.einsum("qhd,kd->hqk", d_head, values, preferred_element_type=F32)
    delta = jnp.sum(soft * d_soft, axis=-1, keepdims=True)
    d_scores = (soft * (d_soft - delta)).astype(BF16)
    d_queries = jnp.einsum("hqk,kd->qhd", d_scores, keys, preferred_element_type=F32)
    d_keys = jnp.einsum("hqk,qhd->kd", d_scores, q_heads, preferred_element_type=F32)
    d_values = jnp.einsum("hqk,qhd->kd", soft.astype(BF16), d_head, preferred_element_type=F32)
    sent = swap_halves(near(jnp.where(core == 0, d_values, d_keys).astype(BF16)))
    d_kv = jnp.where(core == 0, d_keys, d_values) + sent.astype(F32)
    d_kv_pre = jnp.where(core == 0, rotate(d_kv, cosine, -sine), d_kv)
    d_query_pre = rotate(d_queries.reshape(seq_len, q_cols), cosine, -sine) * query_scale
    d_qkv = jnp.concatenate([d_query_pre.astype(BF16), d_kv_pre.astype(BF16)], axis=1)
    grad_qkv = dot(d_qkv, n1, 0, 0).astype(BF16)
    shard_qkv = lax.psum_scatter(grad_qkv, "fsdp", scatter_dimension=1, tiled=True)
    d_n1 = collect(dot(d_qkv, wqkv, 1, 0).astype(BF16))
    inv_one = lax.rsqrt(jnp.mean(x_own * x_own, axis=-1, keepdims=True) + norm_eps)
    hat_one = x_own * inv_one
    input_grad = both_sides((d_mid + norm_back(d_n1, hat_one, inv_one, gain_one)).astype(BF16), t)
    gain_grads = lax.psum(
        jnp.stack([jnp.sum(d_n1 * hat_one, axis=0), jnp.sum(d_n2 * hat_two, axis=0)]),
        ("fsdp", "ctx", "tp"),
    )
    shard_width = gain_attn.shape[0]
    gain_grads = lax.dynamic_slice_in_dim(
        gain_grads, lax.axis_index("fsdp") * shard_width, shard_width, 1
    )
    all_gu = ctx_rows(shard_gu, c)
    all_down = ctx_rows(shard_down, c).reshape(4 * ff, -1)
    all_out = ctx_rows(shard_out, c).reshape(4 * q_cols, -1)
    all_qkv = ctx_rows(shard_qkv, c)
    grad_kv = all_qkv[:, q_cols:].reshape(2, 2, HEAD, -1)
    return (
        output[None],
        input_grad[None],
        all_qkv[:, :q_cols].reshape(4 * q_cols, -1).T.astype(F32),
        grad_kv[:, 0].reshape(2 * HEAD, -1).T.astype(F32),
        grad_kv[:, 1].reshape(2 * HEAD, -1).T.astype(F32),
        all_out.astype(F32),
        all_gu[:, :ff].reshape(4 * ff, -1).T.astype(F32),
        all_gu[:, ff:].reshape(4 * ff, -1).T.astype(F32),
        all_down.astype(F32),
        gain_grads[0],
        gain_grads[1],
    )


def solution(mesh):
    placed = (
        P("fsdp", "ctx", None),
        P("fsdp", None),
        P("fsdp", None),
        P("fsdp", None),
        P("fsdp", "ctx"),
        P("fsdp", "tp"),
        P("fsdp", "tp"),
        P("fsdp", "tp"),
        P("tp", "fsdp"),
        P("fsdp", "tp"),
        P("fsdp", "tp"),
        P("tp", "fsdp"),
        P("fsdp"),
        P("fsdp"),
        P("fsdp", "ctx", None),
    )
    return jax.shard_map(
        body,
        mesh=mesh,
        in_specs=placed,
        out_specs=(
            P("fsdp", "ctx", None),
            P("fsdp", "ctx", None),
            P("fsdp", "tp"),
            P("fsdp", "tp"),
            P("fsdp", "tp"),
            P("tp", "fsdp"),
            P("fsdp", "tp"),
            P("fsdp", "tp"),
            P("tp", "fsdp"),
            P("fsdp"),
            P("fsdp"),
        ),
        check_vma=False,
    )
```

profile of v0, /device:TPU:0, one launch (start us, length us, event | category | flops | bytes accessed | tf_op | source)
XLA Modules:
  0.0 825.5 jit_solution(8399771713944028795)
XLA Ops:
  15.6 3.0 collective-permute-start
  20.2 7.6 collective-permute-done
  31.3 15.3 %collective-permute-done.1 = bf16[384,1024]{1,0:T(8,128)(2,1)S(1)} collective-permute-done((bf16[384,1024]{1,0:T(8,128)(2,1)S(1)}, bf16[384,1024]{1,0:T(8,128)(2,1)S(1)}, u32[]{:S(2)}, u32[]{:S(2)}) %collective-permute-start.1) | collective-permute-done | bytes 786464 | tf_op jit(solution)/shard_map/ppermute | solution.py:64
  47.9 19.6 %maximum_maximum_fusion = bf16[768,2048]{1,0:T(8,128)(2,1)} fusion(bf16[384,1024]{1,0:T(8,128)(2,1)S(1)} %collective-permute-done.3, bf16[192,1024]{1,0:T(8,128)(2,1)S(1)} %collective-permute-done.2, bf16[192,1024]{1,0:T(8,128)(2,1)S(1)} %get-tuple-element.104, bf16[192,1024]{1,0:T(8,128)(2,1)S(1)} %get-tuple-element.102, ...), kind=kLoop, calls=%fused_computation.45 | loop fusion | flops 22020096 | bytes 6291456 | tf_op jit(solution)/shard_map/concatenate | solution.py:76
  69.9 5.5 or_and_fusion
  77.2 6.0 fusion.7
  83.3 3.0 fusion.26
  90.5 5.6 fusion.5
  96.1 6.0 fusion.6
  103.3 8.3 %fusion.16 = bf16[128,2,1536]{2,0,1:T(8,128)(2,1)} fusion(f32[1536,1536,2]{1,0,2:T(8,128)S(1)} %get-tuple-element.123, f32[2,1536]{1,0:T(2,128)S(1)} %fusion.6, f32[2,1536]{1,0:T(2,128)S(1)} %get-tuple-element.122, pred[1536,1536]{0,1:T(8,128)(4,1)} %or_and_fusion, bf16[1536,128]{0,1:T(8,128)(2,1)S(1)} %fusion.55, pred[]{:T(512)S(6)} %eq.48, ...), kind=kOutput, calls=%fused_computation.54 | convolution fusion | flops 1228210176 | bytes 22831104 | tf_op jit(solution)/shard_map/hqk,kd->qhd/dot_general | solution.py:204
  111.5 3.3 convolution_convert_fusion
  114.8 2.7 copy-done.4
  125.6 4.2 add_convert_fusion.3
  132.2 17.4 %collective-permute-done.7 = bf16[384,1024]{1,0:T(8,128)(2,1)S(1)} collective-permute-done((bf16[384,1024]{1,0:T(8,128)(2,1)S(1)}, bf16[384,1024]{1,0:T(8,128)(2,1)S(1)}, u32[]{:S(2)}, u32[]{:S(2)}) %collective-permute-start.7) | collective-permute-done | bytes 786464 | tf_op jit(solution)/shard_map/ppermute | solution.py:56
  152.6 7.9 collective-permute-done.8
  165.9 6.9 collective-permute-done.22
  178.1 15.3 %collective-permute-done.23 = bf16[384,1024]{1,0:T(8,128)(2,1)S(1)} collective-permute-done((bf16[384,1024]{1,0:T(8,128)(2,1)S(1)}, bf16[384,1024]{1,0:T(8,128)(2,1)S(1)}, u32[]{:S(2)}, u32[]{:S(2)}) %collective-permute-start.23) | collective-permute-done | bytes 786464 | tf_op jit(solution)/shard_map/ppermute | solution.py:64
  195.3 19.8 %maximum_maximum_fusion.2 = bf16[768,2048]{1,0:T(8,128)(2,1)} fusion(bf16[384,1024]{1,0:T(8,128)(2,1)S(1)} %collective-permute-done.25, bf16[192,1024]{1,0:T(8,128)(2,1)S(1)} %collective-permute-done.24, bf16[192,1024]{1,0:T(8,128)(2,1)S(1)} %get-tuple-element.96, bf16[192,1024]{1,0:T(8,128)(2,1)S(1)} %get-tuple-element.94, ...), kind=kLoop, calls=%fused_computation.47 | loop fusion | flops 22020096 | bytes 6291456 | tf_op jit(solution)/shard_map/concatenate | solution.py:76
  217.2 18.0 %collective-permute-done.12 = bf16[384,1024]{1,0:T(8,128)(2,1)S(1)} collective-permute-done((bf16[384,1024]{1,0:T(8,128)(2,1)S(1)}, bf16[384,1024]{1,0:T(8,128)(2,1)S(1)}, u32[]{:S(2)}, u32[]{:S(2)}) %collective-permute-start.12) | collective-permute-done | bytes 786464 | tf_op jit(solution)/shard_map/ppermute | solution.py:64
  235.8 20.0 %maximum_maximum_fusion.1 = bf16[768,2048]{1,0:T(8,128)(2,1)} fusion(bf16[384,1024]{1,0:T(8,128)(2,1)S(1)} %collective-permute-done.14, bf16[192,1024]{1,0:T(8,128)(2,1)S(1)} %collective-permute-done.13, bf16[192,1024]{1,0:T(8,128)(2,1)S(1)} %get-tuple-element.100, bf16[192,1024]{1,0:T(8,128)(2,1)S(1)} %get-tuple-element.98, ...), kind=kLoop, calls=%fused_computation.46 | loop fusion | flops 22020096 | bytes 6291456 | tf_op jit(solution)/shard_map/concatenate | solution.py:76
  256.9 7.3 pad_maximum_fusion.2
  264.3 35.1 %fusion.121 = f32[1408,1536]{1,0:T(8,128)} fusion(bf16[1408,2048]{0,1:T(8,128)(2,1)} %all-gather.9.cloned.1.call-done, bf16[768,2048]{1,0:T(8,128)(2,1)} %collective-permute-done.15, bf16[384,1024]{1,0:T(8,128)(2,1)} %copy-done.73, bf16[192,1024]{1,0:T(8,128)(2,1)S(1)} %copy-done.61, bf16[192,1024]{1,0:T(8,128)(2,1)S(1)} %copy-done.42, ...), kind=kOutput, calls=%fused_computation.277 | convolution fusion | flops 8908701696 | bytes 20709376 | tf_op jit(solution)/shard_map/dot_general | solution.py:15
  299.4 17.1 %all-gather.11.cloned.1.call-done = bf16[704,2048]{1,0:T(8,128)(2,1)} async-done(((bf16[704,512]{1,0:T(8,128)(2,1)}), bf16[704,2048]{1,0:T(8,128)(2,1)}) %all-gather.11.cloned.1.call-update) | async-done | bytes 2883600 | tf_op jit(solution)/shard_map/all_gather | solution.py:169
  316.5 13.8 %multiply_convert_fusion.1 = (bf16[704,1536]{1,0:T(8,128)(2,1)S(1)}, bf16[704,1536]{1,0:T(8,128)(2,1)}, bf16[704,1536]{1,0:T(8,128)(2,1)S(1)}) fusion(f32[1408,1536]{1,0:T(8,128)} %fusion.121, bf16[704,2048]{1,0:T(8,128)(2,1)} %all-gather.11.cloned.1.call-done, bf16[1536,2048]{1,0:T(8,128)(2,1)} %pad_maximum_fusion.2), kind=kOutput, calls=%fused_computation.40 | convolution fusion | flops 4445405184 | bytes 24313856 | tf_op jit(solution)/shard_map/dot_general | solution.py:15
  330.3 12.3 %convolution_convert_fusion.3 = bf16[1536,2048]{1,0:T(8,128)(2,1)S(1)} fusion(bf16[1408,2048]{0,1:T(8,128)(2,1)S(1)} %copy-done.93, bf16[704,1536]{1,0:T(8,128)(2,1)} %get-tuple-element.48, bf16[704,1536]{1,0:T(8,128)(2,1)S(1)} %get-tuple-element.47), kind=kOutput, calls=%fused_computation.26 | convolution fusion | flops 8870166528 | bytes 16384000 | tf_op jit(solution)/shard_map/dot_general | solution.py:15
  347.2 5.3 convolution_convert_fusion.4
  356.6 6.4 convolution_convert_fusion.5
  363.1 4.2 add_convert_fusion.1
  370.7 4.2 add_convert_fusion.2
  376.5 11.5 %collective-permute-done.28 = bf16[384,1024]{1,0:T(8,128)(2,1)S(1)} collective-permute-done((bf16[384,1024]{1,0:T(8,128)(2,1)S(1)}, bf16[384,1024]{1,0:T(8,128)(2,1)S(1)}, u32[]{:S(2)}, u32[]{:S(2)}) %collective-permute-start.28) | collective-permute-done | bytes 786464 | tf_op jit(solution)/shard_map/ppermute | solution.py:56
  391.8 13.0 %collective-permute-done.17 = bf16[384,1024]{1,0:T(8,128)(2,1)S(1)} collective-permute-done((bf16[384,1024]{1,0:T(8,128)(2,1)S(1)}, bf16[384,1024]{1,0:T(8,128)(2,1)S(1)}, u32[]{:S(2)}, u32[]{:S(2)}) %collective-permute-start.17) | collective-permute-done | bytes 786464 | tf_op jit(solution)/shard_map/ppermute | solution.py:56
  408.7 6.3 collective-permute-done.29
  417.6 4.5 collective-permute-done.18
  428.4 7.9 collective-permute-done.32
  438.6 15.2 %collective-permute-done.33 = bf16[384,1024]{1,0:T(8,128)(2,1)S(1)} collective-permute-done((bf16[384,1024]{1,0:T(8,128)(2,1)S(1)}, bf16[384,1024]{1,0:T(8,128)(2,1)S(1)}, u32[]{:S(2)}, u32[]{:S(2)}) %collective-permute-start.33) | collective-permute-done | bytes 786464 | tf_op jit(solution)/shard_map/ppermute | solution.py:64
  455.1 19.7 %maximum_maximum_fusion.3 = bf16[768,2048]{1,0:T(8,128)(2,1)} fusion(bf16[384,1024]{1,0:T(8,128)(2,1)S(1)} %collective-permute-done.35, bf16[192,1024]{1,0:T(8,128)(2,1)S(1)} %collective-permute-done.34, bf16[192,1024]{1,0:T(8,128)(2,1)S(1)} %get-tuple-element.92, bf16[192,1024]{1,0:T(8,128)(2,1)S(1)} %get-tuple-element.90, ...), kind=kLoop, calls=%fused_computation.48 | loop fusion | flops 22020096 | bytes 6291456 | tf_op jit(solution)/shard_map/concatenate | solution.py:76
  476.6 17.1 %collective-permute-done.50 = bf16[704,512]{1,0:T(8,128)(2,1)} collective-permute-done((bf16[704,512]{1,0:T(8,128)(2,1)}, bf16[704,512]{1,0:T(8,128)(2,1)}, u32[]{:S(2)}, u32[]{:S(2)}) %collective-permute-start.50) | collective-permute-done | bytes 720928 | tf_op jit(solution)/shard_map/ppermute | solution.py:56
  496.3 5.9 pad_maximum_fusion.3
  502.2 2.7 copy-done.19
  504.9 2.8 convolution_convert_fusion.7
  507.8 16.6 %convolution_convert_fusion.1 = bf16[1408,2048]{1,0:T(8,128)(2,1)} fusion(bf16[704,1536]{1,0:T(8,128)(2,1)} %get-tuple-element.48, bf16[704,1536]{1,0:T(8,128)(2,1)} %copy-done.96, bf16[768,2048]{1,0:T(8,128)(2,1)} %collective-permute-done.15, bf16[384,1024]{1,0:T(8,128)(2,1)} %copy-done.73, bf16[192,1024]{1,0:T(8,128)(2,1)S(1)} %copy-done.62, ...), kind=kOutput, calls=%fused_computation.24 | convolution fusion | flops 8920236032 | bytes 16384000 | tf_op jit(solution)/shard_map/dot_general | solution.py:15
  527.8 3.4 maximum_select_fusion
  542.4 13.2 %fusion = (f32[2,1536]{1,0:T(2,128)S(1)}, f32[1536,1536,2]{1,0,2:T(8,128)}) fusion(f32[1536,1536,2]{1,0,2:T(8,128)} %copy-done.2, f32[2,1536]{1,0:T(2,128)S(1)} %log_add_fusion, pred[1536,1536]{0,1:T(8,128)(4,1)S(1)} %copy-done.3, bf16[1536,2,128]{0,2,1:T(8,128)(2,1)S(1)} %bitcast.232, bf16[1536,128]{0,1:T(8,128)(2,1)S(1)} %copy-done.12, ...), kind=kOutput, calls=%fused_computation.2 | convolution fusion | flops 1227813888 | bytes 41705472 | tf_op jit(solution)/shard_map/qhd,kd->hqk/dot_general | solution.py:236
  555.7 13.7 %fusion.2 = bf16[2,1536,1536]{1,2,0:T(8,128)(2,1)S(1)} fusion(f32[1536,1536,2]{1,0,2:T(8,128)} %get-tuple-element.125, f32[1536,1536,2]{1,0,2:T(8,128)} %copy-done.2, f32[2,1536]{1,0:T(2,128)S(1)} %get-tuple-element.124, f32[2,1536]{1,0:T(2,128)S(1)} %log_add_fusion, pred[1536,1536]{0,1:T(8,128)(4,1)S(1)} %copy-done.3), kind=kLoop, calls=%fused_computation.4 | loop fusion | flops 23592960 | bytes 49569792 | tf_op jit(solution)/shard_map/convert_element_type | solution.py:238
  569.4 4.0 convolution_bitcast_fusion
  573.4 12.0 %select_convert_fusion = (bf16[1536,128]{0,1:T(8,128)(2,1)}, f32[1536,128]{0,1:T(8,128)}) fusion(f32[1536,128]{0,1:T(8,128)} %convolution_bitcast_fusion, pred[]{:T(512)S(6)} %eq.48, bf16[1536,2,128]{0,2,1:T(8,128)(2,1)} %bitcast.233, f32[1536,1536,2]{1,0,2:T(8,128)} %copy-done.2, f32[2,1536]{1,0:T(2,128)S(1)} %log_add_fusion, ...), kind=kOutput, calls=%fused_computation.147 | convolution fusion | flops 1222311936 | bytes 23998464 | tf_op jit(solution)/shard_map/hqk,qhd->kd/dot_general | solution.py:241
  591.6 3.8 convolution_convert_fusion.2
  600.0 6.7 convolution_convert_fusion.6
  608.1 5.2 bitcast_convert_fusion
  613.4 22.9 %reduce-scatter.9.cloned.1.call-done = bf16[1408,512]{1,0:T(8,128)(2,1)} async-done(((bf16[1408,2048]{1,0:T(8,128)(2,1)}), bf16[1408,512]{1,0:T(8,128)(2,1)}) %reduce-scatter.9.cloned.1.call-update) | async-done | bytes 1441808 | tf_op jit(solution)/shard_map/reduce_scatter | solution.py:225
  639.6 3.4 broadcast_in_dim.90
  644.3 3.4 add_convert_fusion
  650.2 25.0 %reduce-scatter.5.cloned.1.call-done = bf16[384,512]{1,0:T(8,128)(2,1)} async-done(((bf16[384,2048]{1,0:T(8,128)(2,1)}), bf16[384,512]{1,0:T(8,128)(2,1)}) %reduce-scatter.5.cloned.1.call-update) | async-done | bytes 393232 | tf_op jit(solution)/shard_map/reduce_scatter | solution.py:248
  678.5 16.7 %collective-permute-done.44 = bf16[384,512]{1,0:T(8,128)(2,1)S(1)} collective-permute-done((bf16[384,512]{1,0:T(8,128)(2,1)}, bf16[384,512]{1,0:T(8,128)(2,1)S(1)}, u32[]{:S(2)}, u32[]{:S(2)}) %collective-permute-start.44) | collective-permute-done | bytes 393248 | tf_op jit(solution)/shard_map/ppermute | solution.py:56
  696.3 3.8 pad_maximum_fusion.5
  708.4 5.1 collective-permute-done.40
  718.9 51.3 %psum.7 = f32[2,2048]{1,0:T(2,128)S(1)} all-reduce(f32[2,2048]{1,0:T(2,128)S(1)} %pad_maximum_fusion.26), channel_id=1, replica_groups=mesh['fsdp'=4,'ctx'=4,'tp'=2] {'fsdp','ctx','tp'}, use_global_device_ids=true, to_apply=%region_15.16 | all-reduce | flops 4096 | bytes 32768 | tf_op jit(solution)/shard_map/psum | solution.py:253
  770.9 4.5 fusion.32
  784.1 3.2 maximum_select_fusion.1
  792.5 4.7 fusion.123
  797.2 3.5 convert_bitcast_fusion
  800.7 6.2 copy.72
  806.9 5.2 convert_bitcast_fusion.1
  812.2 6.2 copy.71
  (457 shorter events, 158.0 us)
Async XLA Ops:
  7.2 248.6 %copy-start = (bf16[2816,512]{1,0:T(8,128)(2,1)S(1)}, bf16[2816,512]{1,0:T(8,128)(2,1)}, u32[]{:S(2)}) copy-start(bf16[2816,512]{1,0:T(8,128)(2,1)} %param.26) | copy-start | bytes 8650756
  7.2 68.2 %all-gather.5.cloned.1.call-start = ((), (), s32[]{:S(2)}) async-start(), calls=%async_computation.4 | async-start | bytes 2621440 | tf_op jit(solution)/shard_map/all_gather | solution.py:156
  13.6 98.0 %all-gather.7.cloned.1.call-start = ((), (), s32[]{:S(2)}) async-start(), calls=%async_computation.5 | async-start | bytes 1310720 | tf_op jit(solution)/shard_map/all_gather | solution.py:163
  15.6 12.1 %collective-permute-start = (bf16[192,1024]{1,0:T(8,128)(2,1)S(1)}, bf16[192,1024]{1,0:T(8,128)(2,1)S(1)}, u32[]{:S(2)}, u32[]{:S(2)}) collective-permute-start(bf16[192,1024]{1,0:T(8,128)(2,1)S(1)} %get-tuple-element.103), channel_id=1, source_target_pairs={{0,4},{2,6},{4,0},{6,2},{1,5},{3,7},{5,1},{7,3},{8,12},{10,14},{12... | collective-permute-start | bytes 1179656 | tf_op jit(solution)/shard_map/ppermute | solution.py:56
  18.6 11.0 %collective-permute-start.2 = (bf16[192,1024]{1,0:T(8,128)(2,1)S(1)}, bf16[192,1024]{1,0:T(8,128)(2,1)S(1)}, u32[]{:S(2)}, u32[]{:S(2)}) collective-permute-start(bf16[192,1024]{1,0:T(8,128)(2,1)S(1)} %get-tuple-element.104), channel_id=1, source_target_pairs={{0,1},{1,0},{2,3},{3,2},{4,5},{5,4},{6,7},{7,6},{8,9},{9,8},{10,11... | collective-permute-start | bytes 1179656 | tf_op jit(solution)/shard_map/ppermute | solution.py:64
  27.8 18.8 %collective-permute-start.1 = (bf16[384,1024]{1,0:T(8,128)(2,1)S(1)}, bf16[384,1024]{1,0:T(8,128)(2,1)S(1)}, u32[]{:S(2)}, u32[]{:S(2)}) collective-permute-start(bf16[384,1024]{1,0:T(8,128)(2,1)S(1)} %pad_maximum_fusion.13), channel_id=1, source_target_pairs={{0,1},{1,0},{2,3},{3,2},{4,5},{5,4},{6,7},{7,6},{8,9},{9,8},{10,11... | collective-permute-start | bytes 2359304 | tf_op jit(solution)/shard_map/ppermute | solution.py:64
  29.7 18.2 %collective-permute-start.3 = (bf16[384,1024]{1,0:T(8,128)(2,1)S(1)}, bf16[384,1024]{1,0:T(8,128)(2,1)S(1)}, u32[]{:S(2)}, u32[]{:S(2)}) collective-permute-start(bf16[384,1024]{1,0:T(8,128)(2,1)S(1)} %pad_maximum_fusion.14), channel_id=1, source_target_pairs={{0,4},{2,6},{4,0},{6,2},{1,5},{3,7},{5,1},{7,3},{8,12},{10,14},{12... | collective-permute-start | bytes 2359304 | tf_op jit(solution)/shard_map/ppermute | solution.py:56
  67.5 9.7 %collective-permute-start.4 = (bf16[768,2048]{1,0:T(8,128)(2,1)}, bf16[768,2048]{1,0:T(8,128)(2,1)}, u32[]{:S(2)}, u32[]{:S(2)}) collective-permute-start(bf16[768,2048]{1,0:T(8,128)(2,1)} %maximum_maximum_fusion), channel_id=1, source_target_pairs={{0,2},{2,0},{4,6},{6,4},{1,3},{3,1},{5,7},{7,5},{8,10},{10,8},{12,... | collective-permute-start | bytes 9437192 | tf_op jit(solution)/shard_map/ppermute | solution.py:60
  69.3 194.9 %all-gather.9.cloned.1.call-start = ((), (), s32[]{:S(2)}) async-start(), calls=%async_computation.6 | async-start | bytes 7208960 | tf_op jit(solution)/shard_map/all_gather | solution.py:168
  88.1 2.4 collective-permute-start.5
  119.6 6.0 collective-permute-start.6
  123.4 193.1 %all-gather.11.cloned.1.call-start = ((), (), s32[]{:S(2)}) async-start(), calls=%async_computation.7 | async-start | bytes 3604480 | tf_op jit(solution)/shard_map/all_gather | solution.py:169
  130.0 19.6 %collective-permute-start.7 = (bf16[384,1024]{1,0:T(8,128)(2,1)S(1)}, bf16[384,1024]{1,0:T(8,128)(2,1)S(1)}, u32[]{:S(2)}, u32[]{:S(2)}) collective-permute-start(bf16[384,1024]{1,0:T(8,128)(2,1)S(1)} %slice.429), channel_id=1, source_target_pairs={{0,4},{2,6},{4,0},{6,2},{1,5},{3,7},{5,1},{7,3},{8,12},{10,14},{12... | collective-permute-start | bytes 2359304 | tf_op jit(solution)/shard_map/ppermute | solution.py:56
  131.7 19.5 %collective-permute-start.9 = (bf16[384,1024]{1,0:T(8,128)(2,1)S(1)}, bf16[384,1024]{1,0:T(8,128)(2,1)S(1)}, u32[]{:S(2)}, u32[]{:S(2)}) collective-permute-start(bf16[384,1024]{1,0:T(8,128)(2,1)S(1)} %bitcast.231), channel_id=1, source_target_pairs={{0,1},{1,0},{2,3},{3,2},{4,5},{5,4},{6,7},{7,6},{8,9},{9,8},{10,11... | collective-permute-start | bytes 2359304 | tf_op jit(solution)/shard_map/ppermute | solution.py:64
  150.0 10.5 %collective-permute-start.8 = (bf16[192,1024]{1,0:T(8,128)(2,1)S(1)}, bf16[192,1024]{1,0:T(8,128)(2,1)S(1)}, u32[]{:S(2)}, u32[]{:S(2)}) collective-permute-start(bf16[192,1024]{1,0:T(8,128)(2,1)S(1)} %slice.431), channel_id=1, source_target_pairs={{0,1},{1,0},{2,3},{3,2},{4,5},{5,4},{6,7},{7,6},{8,9},{9,8},{10,11... | collective-permute-start | bytes 1179656 | tf_op jit(solution)/shard_map/ppermute | solution.py:64
  151.6 10.2 %collective-permute-start.10 = (bf16[192,1024]{1,0:T(8,128)(2,1)S(1)}, bf16[192,1024]{1,0:T(8,128)(2,1)S(1)}, u32[]{:S(2)}, u32[]{:S(2)}) collective-permute-start(bf16[192,1024]{1,0:T(8,128)(2,1)S(1)} %slice.436), channel_id=1, source_target_pairs={{0,4},{2,6},{4,0},{6,2},{1,5},{3,7},{5,1},{7,3},{8,12},{10,14},{12... | collective-permute-start | bytes 1179656 | tf_op jit(solution)/shard_map/ppermute | solution.py:56
  163.4 9.4 %collective-permute-start.22 = (bf16[192,1024]{1,0:T(8,128)(2,1)S(1)}, bf16[192,1024]{1,0:T(8,128)(2,1)S(1)}, u32[]{:S(2)}, u32[]{:S(2)}) collective-permute-start(bf16[192,1024]{1,0:T(8,128)(2,1)S(1)} %get-tuple-element.95), channel_id=1, source_target_pairs={{0,4},{2,6},{4,0},{6,2},{1,5},{3,7},{5,1},{7,3},{8,12},{10,14},{12... | collective-permute-start | bytes 1179656 | tf_op jit(solution)/shard_map/ppermute | solution.py:56
  164.6 10.3 %collective-permute-start.24 = (bf16[192,1024]{1,0:T(8,128)(2,1)S(1)}, bf16[192,1024]{1,0:T(8,128)(2,1)S(1)}, u32[]{:S(2)}, u32[]{:S(2)}) collective-permute-start(bf16[192,1024]{1,0:T(8,128)(2,1)S(1)} %get-tuple-element.96), channel_id=1, source_target_pairs={{0,1},{1,0},{2,3},{3,2},{4,5},{5,4},{6,7},{7,6},{8,9},{9,8},{10,11... | collective-permute-start | bytes 1179656 | tf_op jit(solution)/shard_map/ppermute | solution.py:64
  172.8 20.5 %collective-permute-start.23 = (bf16[384,1024]{1,0:T(8,128)(2,1)S(1)}, bf16[384,1024]{1,0:T(8,128)(2,1)S(1)}, u32[]{:S(2)}, u32[]{:S(2)}) collective-permute-start(bf16[384,1024]{1,0:T(8,128)(2,1)S(1)} %pad_maximum_fusion.17), channel_id=1, source_target_pairs={{0,1},{1,0},{2,3},{3,2},{4,5},{5,4},{6,7},{7,6},{8,9},{9,8},{10,11... | collective-permute-start | bytes 2359304 | tf_op jit(solution)/shard_map/ppermute | solution.py:64
  175.0 20.3 %collective-permute-start.25 = (bf16[384,1024]{1,0:T(8,128)(2,1)S(1)}, bf16[384,1024]{1,0:T(8,128)(2,1)S(1)}, u32[]{:S(2)}, u32[]{:S(2)}) collective-permute-start(bf16[384,1024]{1,0:T(8,128)(2,1)S(1)} %pad_maximum_fusion.18), channel_id=1, source_target_pairs={{0,4},{2,6},{4,0},{6,2},{1,5},{3,7},{5,1},{7,3},{8,12},{10,14},{12... | collective-permute-start | bytes 2359304 | tf_op jit(solution)/shard_map/ppermute | solution.py:56
  175.7 60.0 %copy-start.39 = (bf16[192,1024]{1,0:T(8,128)(2,1)}, bf16[192,1024]{1,0:T(8,128)(2,1)S(1)}, u32[]{:S(2)}) copy-start(bf16[192,1024]{1,0:T(8,128)(2,1)S(1)} %get-tuple-element.99) | copy-start | bytes 1179652
  175.7 60.0 %copy-start.41 = (bf16[192,1024]{1,0:T(8,128)(2,1)}, bf16[192,1024]{1,0:T(8,128)(2,1)S(1)}, u32[]{:S(2)}) copy-start(bf16[192,1024]{1,0:T(8,128)(2,1)S(1)} %get-tuple-element.100) | copy-start | bytes 1179652
  175.8 39.4 %collective-permute-start.11 = (bf16[192,1024]{1,0:T(8,128)(2,1)S(1)}, bf16[192,1024]{1,0:T(8,128)(2,1)S(1)}, u32[]{:S(2)}, u32[]{:S(2)}) collective-permute-start(bf16[192,1024]{1,0:T(8,128)(2,1)S(1)} %get-tuple-element.99), channel_id=1, source_target_pairs={{0,4},{2,6},{4,0},{6,2},{1,5},{3,7},{5,1},{7,3},{8,12},{10,14},{12... | collective-permute-start | bytes 1179656 | tf_op jit(solution)/shard_map/ppermute | solution.py:56
  177.4 38.6 %collective-permute-start.13 = (bf16[192,1024]{1,0:T(8,128)(2,1)S(1)}, bf16[192,1024]{1,0:T(8,128)(2,1)S(1)}, u32[]{:S(2)}, u32[]{:S(2)}) collective-permute-start(bf16[192,1024]{1,0:T(8,128)(2,1)S(1)} %get-tuple-element.100), channel_id=1, source_target_pairs={{0,1},{1,0},{2,3},{3,2},{4,5},{5,4},{6,7},{7,6},{8,9},{9,8},{10,11... | collective-permute-start | bytes 1179656 | tf_op jit(solution)/shard_map/ppermute | solution.py:64
  215.1 41.8 %collective-permute-start.26 = (bf16[768,2048]{1,0:T(8,128)(2,1)}, bf16[768,2048]{1,0:T(8,128)(2,1)}, u32[]{:S(2)}, u32[]{:S(2)}) collective-permute-start(bf16[768,2048]{1,0:T(8,128)(2,1)} %maximum_maximum_fusion.2), channel_id=1, source_target_pairs={{0,2},{2,0},{4,6},{6,4},{1,3},{3,1},{5,7},{7,5},{8,10},{10,8},{12,... | collective-permute-start | bytes 9437192 | tf_op jit(solution)/shard_map/ppermute | solution.py:60
  215.2 20.0 %collective-permute-start.12 = (bf16[384,1024]{1,0:T(8,128)(2,1)S(1)}, bf16[384,1024]{1,0:T(8,128)(2,1)S(1)}, u32[]{:S(2)}, u32[]{:S(2)}) collective-permute-start(bf16[384,1024]{1,0:T(8,128)(2,1)S(1)} %pad_maximum_fusion.15), channel_id=1, source_target_pairs={{0,1},{1,0},{2,3},{3,2},{4,5},{5,4},{6,7},{7,6},{8,9},{9,8},{10,11... | collective-permute-start | bytes 2359304 | tf_op jit(solution)/shard_map/ppermute | solution.py:64
  216.0 19.7 %collective-permute-start.14 = (bf16[384,1024]{1,0:T(8,128)(2,1)S(1)}, bf16[384,1024]{1,0:T(8,128)(2,1)S(1)}, u32[]{:S(2)}, u32[]{:S(2)}) collective-permute-start(bf16[384,1024]{1,0:T(8,128)(2,1)S(1)} %pad_maximum_fusion.16), channel_id=1, source_target_pairs={{0,4},{2,6},{4,0},{6,2},{1,5},{3,7},{5,1},{7,3},{8,12},{10,14},{12... | collective-permute-start | bytes 2359304 | tf_op jit(solution)/shard_map/ppermute | solution.py:56
  255.7 8.5 %collective-permute-start.15 = (bf16[768,2048]{1,0:T(8,128)(2,1)}, bf16[768,2048]{1,0:T(8,128)(2,1)}, u32[]{:S(2)}, u32[]{:S(2)}) collective-permute-start(bf16[768,2048]{1,0:T(8,128)(2,1)} %maximum_maximum_fusion.1), channel_id=1, source_target_pairs={{0,2},{2,0},{4,6},{6,4},{1,3},{3,1},{5,7},{7,5},{8,10},{10,8},{12,... | collective-permute-start | bytes 9437192 | tf_op jit(solution)/shard_map/ppermute | solution.py:60
  256.8 218.0 %reduce-scatter.11.cloned.1.call-start = ((), (), s32[]{:S(2)}) async-start(), calls=%async_computation.11 | async-start | bytes 3604480 | tf_op jit(solution)/shard_map/reduce_scatter | solution.py:226
  347.2 15.9 %collective-permute-start.27 = (bf16[768,2048]{1,0:T(8,128)(2,1)}, bf16[768,2048]{1,0:T(8,128)(2,1)}, u32[]{:S(2)}, u32[]{:S(2)}) collective-permute-start(bf16[768,2048]{1,0:T(8,128)(2,1)} %slice.460), channel_id=1, source_target_pairs={{0,2},{2,0},{4,6},{6,4},{1,3},{3,1},{5,7},{7,5},{8,10},{10,8},{12,... | collective-permute-start | bytes 9437192 | tf_op jit(solution)/shard_map/ppermute | solution.py:60
  356.1 14.6 %collective-permute-start.16 = (bf16[768,2048]{1,0:T(8,128)(2,1)}, bf16[768,2048]{1,0:T(8,128)(2,1)}, u32[]{:S(2)}, u32[]{:S(2)}) collective-permute-start(bf16[768,2048]{1,0:T(8,128)(2,1)} %slice.445), channel_id=1, source_target_pairs={{0,2},{2,0},{4,6},{6,4},{1,3},{3,1},{5,7},{7,5},{8,10},{10,8},{12,... | collective-permute-start | bytes 9437192 | tf_op jit(solution)/shard_map/ppermute | solution.py:60
  363.1 236.0 %reduce-scatter.7.cloned.1.call-start = ((), (), s32[]{:S(2)}) async-start(), calls=%async_computation.9 | async-start | bytes 1310720 | tf_op jit(solution)/shard_map/reduce_scatter | solution.py:232
  367.5 20.5 %collective-permute-start.28 = (bf16[384,1024]{1,0:T(8,128)(2,1)S(1)}, bf16[384,1024]{1,0:T(8,128)(2,1)S(1)}, u32[]{:S(2)}, u32[]{:S(2)}) collective-permute-start(bf16[384,1024]{1,0:T(8,128)(2,1)S(1)} %slice.462), channel_id=1, source_target_pairs={{0,4},{2,6},{4,0},{6,2},{1,5},{3,7},{5,1},{7,3},{8,12},{10,14},{12... | collective-permute-start | bytes 2359304 | tf_op jit(solution)/shard_map/ppermute | solution.py:56
  369.2 20.7 %collective-permute-start.30 = (bf16[384,1024]{1,0:T(8,128)(2,1)S(1)}, bf16[384,1024]{1,0:T(8,128)(2,1)S(1)}, u32[]{:S(2)}, u32[]{:S(2)}) collective-permute-start(bf16[384,1024]{1,0:T(8,128)(2,1)S(1)} %bitcast.230), channel_id=1, source_target_pairs={{0,1},{1,0},{2,3},{3,2},{4,5},{5,4},{6,7},{7,6},{8,9},{9,8},{10,11... | collective-permute-start | bytes 2359304 | tf_op jit(solution)/shard_map/ppermute | solution.py:64
  375.1 29.7 %collective-permute-start.17 = (bf16[384,1024]{1,0:T(8,128)(2,1)S(1)}, bf16[384,1024]{1,0:T(8,128)(2,1)S(1)}, u32[]{:S(2)}, u32[]{:S(2)}) collective-permute-start(bf16[384,1024]{1,0:T(8,128)(2,1)S(1)} %slice.447), channel_id=1, source_target_pairs={{0,4},{2,6},{4,0},{6,2},{1,5},{3,7},{5,1},{7,3},{8,12},{10,14},{12... | collective-permute-start | bytes 2359304 | tf_op jit(solution)/shard_map/ppermute | solution.py:56
  375.9 30.9 %collective-permute-start.19 = (bf16[384,1024]{1,0:T(8,128)(2,1)S(1)}, bf16[384,1024]{1,0:T(8,128)(2,1)S(1)}, u32[]{:S(2)}, u32[]{:S(2)}) collective-permute-start(bf16[384,1024]{1,0:T(8,128)(2,1)S(1)} %bitcast.229), channel_id=1, source_target_pairs={{0,1},{1,0},{2,3},{3,2},{4,5},{5,4},{6,7},{7,6},{8,9},{9,8},{10,11... | collective-permute-start | bytes 2359304 | tf_op jit(solution)/shard_map/ppermute | solution.py:64
  388.4 26.6 %collective-permute-start.29 = (bf16[192,1024]{1,0:T(8,128)(2,1)S(1)}, bf16[192,1024]{1,0:T(8,128)(2,1)S(1)}, u32[]{:S(2)}, u32[]{:S(2)}) collective-permute-start(bf16[192,1024]{1,0:T(8,128)(2,1)S(1)} %slice.464), channel_id=1, source_target_pairs={{0,1},{1,0},{2,3},{3,2},{4,5},{5,4},{6,7},{7,6},{8,9},{9,8},{10,11... | collective-permute-start | bytes 1179656 | tf_op jit(solution)/shard_map/ppermute | solution.py:64
  390.3 25.8 %collective-permute-start.31 = (bf16[192,1024]{1,0:T(8,128)(2,1)S(1)}, bf16[192,1024]{1,0:T(8,128)(2,1)S(1)}, u32[]{:S(2)}, u32[]{:S(2)}) collective-permute-start(bf16[192,1024]{1,0:T(8,128)(2,1)S(1)} %slice.469), channel_id=1, source_target_pairs={{0,4},{2,6},{4,0},{6,2},{1,5},{3,7},{5,1},{7,3},{8,12},{10,14},{12... | collective-permute-start | bytes 1179656 | tf_op jit(solution)/shard_map/ppermute | solution.py:56
  405.2 17.0 %collective-permute-start.18 = (bf16[192,1024]{1,0:T(8,128)(2,1)S(1)}, bf16[192,1024]{1,0:T(8,128)(2,1)S(1)}, u32[]{:S(2)}, u32[]{:S(2)}) collective-permute-start(bf16[192,1024]{1,0:T(8,128)(2,1)S(1)} %slice.449), channel_id=1, source_target_pairs={{0,1},{1,0},{2,3},{3,2},{4,5},{5,4},{6,7},{7,6},{8,9},{9,8},{10,11... | collective-permute-start | bytes 1179656 | tf_op jit(solution)/shard_map/ppermute | solution.py:64
  407.2 16.1 %collective-permute-start.20 = (bf16[192,1024]{1,0:T(8,128)(2,1)S(1)}, bf16[192,1024]{1,0:T(8,128)(2,1)S(1)}, u32[]{:S(2)}, u32[]{:S(2)}) collective-permute-start(bf16[192,1024]{1,0:T(8,128)(2,1)S(1)} %slice.454), channel_id=1, source_target_pairs={{0,4},{2,6},{4,0},{6,2},{1,5},{3,7},{5,1},{7,3},{8,12},{10,14},{12... | collective-permute-start | bytes 1179656 | tf_op jit(solution)/shard_map/ppermute | solution.py:56
  426.3 10.0 %collective-permute-start.32 = (bf16[192,1024]{1,0:T(8,128)(2,1)S(1)}, bf16[192,1024]{1,0:T(8,128)(2,1)S(1)}, u32[]{:S(2)}, u32[]{:S(2)}) collective-permute-start(bf16[192,1024]{1,0:T(8,128)(2,1)S(1)} %get-tuple-element.91), channel_id=1, source_target_pairs={{0,4},{2,6},{4,0},{6,2},{1,5},{3,7},{5,1},{7,3},{8,12},{10,14},{12... | collective-permute-start | bytes 1179656 | tf_op jit(solution)/shard_map/ppermute | solution.py:56
  426.9 10.9 %collective-permute-start.34 = (bf16[192,1024]{1,0:T(8,128)(2,1)S(1)}, bf16[192,1024]{1,0:T(8,128)(2,1)S(1)}, u32[]{:S(2)}, u32[]{:S(2)}) collective-permute-start(bf16[192,1024]{1,0:T(8,128)(2,1)S(1)} %get-tuple-element.92), channel_id=1, source_target_pairs={{0,1},{1,0},{2,3},{3,2},{4,5},{5,4},{6,7},{7,6},{8,9},{9,8},{10,11... | collective-permute-start | bytes 1179656 | tf_op jit(solution)/shard_map/ppermute | solution.py:64
  436.3 17.5 %collective-permute-start.33 = (bf16[384,1024]{1,0:T(8,128)(2,1)S(1)}, bf16[384,1024]{1,0:T(8,128)(2,1)S(1)}, u32[]{:S(2)}, u32[]{:S(2)}) collective-permute-start(bf16[384,1024]{1,0:T(8,128)(2,1)S(1)} %pad_maximum_fusion.19), channel_id=1, source_target_pairs={{0,1},{1,0},{2,3},{3,2},{4,5},{5,4},{6,7},{7,6},{8,9},{9,8},{10,11... | collective-permute-start | bytes 2359304 | tf_op jit(solution)/shard_map/ppermute | solution.py:64
  437.9 17.2 %collective-permute-start.35 = (bf16[384,1024]{1,0:T(8,128)(2,1)S(1)}, bf16[384,1024]{1,0:T(8,128)(2,1)S(1)}, u32[]{:S(2)}, u32[]{:S(2)}) collective-permute-start(bf16[384,1024]{1,0:T(8,128)(2,1)S(1)} %pad_maximum_fusion.20), channel_id=1, source_target_pairs={{0,4},{2,6},{4,0},{6,2},{1,5},{3,7},{5,1},{7,3},{8,12},{10,14},{12... | collective-permute-start | bytes 2359304 | tf_op jit(solution)/shard_map/ppermute | solution.py:56
  474.8 21.4 %collective-permute-start.36 = (bf16[768,2048]{1,0:T(8,128)(2,1)}, bf16[768,2048]{1,0:T(8,128)(2,1)}, u32[]{:S(2)}, u32[]{:S(2)}) collective-permute-start(bf16[768,2048]{1,0:T(8,128)(2,1)} %maximum_maximum_fusion.3), channel_id=1, source_target_pairs={{0,2},{2,0},{4,6},{6,4},{1,3},{3,1},{5,7},{7,5},{8,10},{10,8},{12,... | collective-permute-start | bytes 9437192 | tf_op jit(solution)/shard_map/ppermute | solution.py:60
  474.8 18.9 %collective-permute-start.50 = (bf16[704,512]{1,0:T(8,128)(2,1)}, bf16[704,512]{1,0:T(8,128)(2,1)}, u32[]{:S(2)}, u32[]{:S(2)}) collective-permute-start(bf16[704,512]{1,0:T(8,128)(2,1)} %reduce-scatter.11.cloned.1.call-done), channel_id=1, source_target_pairs={{0,4},{2,6},{4,0},{6,2},{1,5},{3,7},{5,1},{7,3},{8,12},{10,14},{12... | collective-permute-start | bytes 2162696 | tf_op jit(solution)/shard_map/ppermute | solution.py:56
  475.5 52.4 %collective-permute-start.21 = (bf16[192,2048]{1,0:T(8,128)(2,1)}, bf16[192,2048]{1,0:T(8,128)(2,1)}, u32[]{:S(2)}, u32[]{:S(2)}) collective-permute-start(bf16[192,2048]{1,0:T(8,128)(2,1)} %get-tuple-element.62), channel_id=1, source_target_pairs={{0,1},{1,0},{2,3},{3,2},{4,5},{5,4},{6,7},{7,6},{8,9},{9,8},{10,11... | collective-permute-start | bytes 2359304 | tf_op jit(solution)/shard_map/ppermute | solution.py:64
  496.2 39.9 %collective-permute-start.51 = (bf16[2,704,512]{2,1,0:T(8,128)(2,1)}, bf16[2,704,512]{2,1,0:T(8,128)(2,1)}, u32[]{:S(2)}, u32[]{:S(2)}) collective-permute-start(bf16[2,704,512]{2,1,0:T(8,128)(2,1)} %pad_maximum_fusion.11), channel_id=1, source_target_pairs={{0,2},{2,0},{4,6},{6,4},{1,3},{3,1},{5,7},{7,5},{8,10},{10,8},{12,... | collective-permute-start | bytes 4325384 | tf_op jit(solution)/shard_map/ppermute | solution.py:60
  507.7 128.7 %reduce-scatter.9.cloned.1.call-start = ((), (), s32[]{:S(2)}) async-start(), calls=%async_computation.10 | async-start | bytes 7208960 | tf_op jit(solution)/shard_map/reduce_scatter | solution.py:225
  524.4 150.8 %reduce-scatter.5.cloned.1.call-start = ((), (), s32[]{:S(2)}) async-start(), calls=%async_computation.8 | async-start | bytes 1966080 | tf_op jit(solution)/shard_map/reduce_scatter | solution.py:248
  585.4 4.1 collective-permute-start.37
  599.0 45.2 %collective-permute-start.38 = (bf16[768,2048]{1,0:T(8,128)(2,1)}, bf16[768,2048]{1,0:T(8,128)(2,1)}, u32[]{:S(2)}, u32[]{:S(2)}) collective-permute-start(bf16[768,2048]{1,0:T(8,128)(2,1)} %slice.483), channel_id=1, source_target_pairs={{0,2},{2,0},{4,6},{6,4},{1,3},{3,1},{5,7},{7,5},{8,10},{10,8},{12,... | collective-permute-start | bytes 9437192 | tf_op jit(solution)/shard_map/ppermute | solution.py:60
  599.0 8.9 %collective-permute-start.46 = (bf16[256,512]{1,0:T(8,128)(2,1)}, bf16[256,512]{1,0:T(8,128)(2,1)S(1)}, u32[]{:S(2)}, u32[]{:S(2)}) collective-permute-start(bf16[256,512]{1,0:T(8,128)(2,1)} %reduce-scatter.7.cloned.1.call-done), channel_id=1, source_target_pairs={{0,4},{2,6},{4,0},{6,2},{1,5},{3,7},{5,1},{7,3},{8,12},{10,14},{12... | collective-permute-start | bytes 786440 | tf_op jit(solution)/shard_map/ppermute | solution.py:56
  608.0 29.8 %collective-permute-start.47 = (bf16[2,256,512]{2,1,0:T(8,128)(2,1)S(1)}, bf16[2,256,512]{2,1,0:T(8,128)(2,1)S(1)}, u32[]{:S(2)}, u32[]{:S(2)}) collective-permute-start(bf16[2,256,512]{2,1,0:T(8,128)(2,1)S(1)} %pad_maximum_fusion.24), channel_id=1, source_target_pairs={{0,2},{2,0},{4,6},{6,4},{1,3},{3,1},{5,7},{7,5},{8,10},{10,8},{12,... | collective-permute-start | bytes 1572872 | tf_op jit(solution)/shard_map/ppermute | solution.py:60
  636.3 59.9 %collective-permute-start.48 = (bf16[1408,512]{1,0:T(8,128)(2,1)}, bf16[1408,512]{1,0:T(8,128)(2,1)}, u32[]{:S(2)}, u32[]{:S(2)}) collective-permute-start(bf16[1408,512]{1,0:T(8,128)(2,1)} %reduce-scatter.9.cloned.1.call-done), channel_id=1, source_target_pairs={{0,4},{2,6},{4,0},{6,2},{1,5},{3,7},{5,1},{7,3},{8,12},{10,14},{12... | collective-permute-start | bytes 4325384 | tf_op jit(solution)/shard_map/ppermute | solution.py:56
  649.8 50.8 %collective-permute-start.39 = (bf16[384,1024]{1,0:T(8,128)(2,1)}, bf16[384,1024]{1,0:T(8,128)(2,1)}, u32[]{:S(2)}, u32[]{:S(2)}) collective-permute-start(bf16[384,1024]{1,0:T(8,128)(2,1)} %slice.485), channel_id=1, source_target_pairs={{0,4},{2,6},{4,0},{6,2},{1,5},{3,7},{5,1},{7,3},{8,12},{10,14},{12... | collective-permute-start | bytes 2359304 | tf_op jit(solution)/shard_map/ppermute | solution.py:56
  675.2 20.0 %collective-permute-start.44 = (bf16[384,512]{1,0:T(8,128)(2,1)}, bf16[384,512]{1,0:T(8,128)(2,1)S(1)}, u32[]{:S(2)}, u32[]{:S(2)}) collective-permute-start(bf16[384,512]{1,0:T(8,128)(2,1)} %reduce-scatter.5.cloned.1.call-done), channel_id=1, source_target_pairs={{0,4},{2,6},{4,0},{6,2},{1,5},{3,7},{5,1},{7,3},{8,12},{10,14},{12... | collective-permute-start | bytes 1179656 | tf_op jit(solution)/shard_map/ppermute | solution.py:56
  676.8 27.1 %collective-permute-start.41 = (bf16[384,1024]{1,0:T(8,128)(2,1)S(1)}, bf16[384,1024]{1,0:T(8,128)(2,1)S(1)}, u32[]{:S(2)}, u32[]{:S(2)}) collective-permute-start(bf16[384,1024]{1,0:T(8,128)(2,1)S(1)} %bitcast.228), channel_id=1, source_target_pairs={{0,1},{1,0},{2,3},{3,2},{4,5},{5,4},{6,7},{7,6},{8,9},{9,8},{10,11... | collective-permute-start | bytes 2359304 | tf_op jit(solution)/shard_map/ppermute | solution.py:64
  696.2 79.2 %collective-permute-start.45 = (bf16[2,384,512]{2,1,0:T(8,128)(2,1)}, bf16[2,384,512]{2,1,0:T(8,128)(2,1)}, u32[]{:S(2)}, u32[]{:S(2)}) collective-permute-start(bf16[2,384,512]{2,1,0:T(8,128)(2,1)} %pad_maximum_fusion.21), channel_id=1, source_target_pairs={{0,2},{2,0},{4,6},{6,4},{1,3},{3,1},{5,7},{7,5},{8,10},{10,8},{12,... | collective-permute-start | bytes 2359304 | tf_op jit(solution)/shard_map/ppermute | solution.py:60
  700.1 87.2 %collective-permute-start.49 = (bf16[2,1408,512]{2,1,0:T(8,128)(2,1)}, bf16[2,1408,512]{2,1,0:T(8,128)(2,1)}, u32[]{:S(2)}, u32[]{:S(2)}) collective-permute-start(bf16[2,1408,512]{2,1,0:T(8,128)(2,1)} %pad_maximum_fusion.5), channel_id=1, source_target_pairs={{0,2},{2,0},{4,6},{6,4},{1,3},{3,1},{5,7},{7,5},{8,10},{10,8},{12,... | collective-permute-start | bytes 8650760 | tf_op jit(solution)/shard_map/ppermute | solution.py:60
  702.3 11.1 %collective-permute-start.40 = (bf16[192,1024]{1,0:T(8,128)(2,1)S(1)}, bf16[192,1024]{1,0:T(8,128)(2,1)S(1)}, u32[]{:S(2)}, u32[]{:S(2)}) collective-permute-start(bf16[192,1024]{1,0:T(8,128)(2,1)S(1)} %slice.487), channel_id=1, source_target_pairs={{0,1},{1,0},{2,3},{3,2},{4,5},{5,4},{6,7},{7,6},{8,9},{9,8},{10,11... | collective-permute-start | bytes 1179656 | tf_op jit(solution)/shard_map/ppermute | solution.py:64
  704.3 10.8 %collective-permute-start.42 = (bf16[192,1024]{1,0:T(8,128)(2,1)S(1)}, bf16[192,1024]{1,0:T(8,128)(2,1)S(1)}, u32[]{:S(2)}, u32[]{:S(2)}) collective-permute-start(bf16[192,1024]{1,0:T(8,128)(2,1)S(1)} %slice.492), channel_id=1, source_target_pairs={{0,4},{2,6},{4,0},{6,2},{1,5},{3,7},{5,1},{7,3},{8,12},{10,14},{12... | collective-permute-start | bytes 1179656 | tf_op jit(solution)/shard_map/ppermute | solution.py:56
  716.1 54.8 %copy-start.16 = (f32[1,192,1024]{2,1,0:T(8,128)S(1)}, f32[1,192,1024]{2,1,0:T(8,128)}, u32[]{:S(2)}) copy-start(f32[1,192,1024]{2,1,0:T(8,128)} %get-tuple-element.81) | copy-start | bytes 2359300
  718.1 66.0 %collective-permute-start.43 = (bf16[192,2048]{1,0:T(8,128)(2,1)}, bf16[192,2048]{1,0:T(8,128)(2,1)}, u32[]{:S(2)}, u32[]{:S(2)}) collective-permute-start(bf16[192,2048]{1,0:T(8,128)(2,1)} %fusion.38), channel_id=1, source_target_pairs={{0,1},{1,0},{2,3},{3,2},{4,5},{5,4},{6,7},{7,6},{8,9},{9,8},{10,11... | collective-permute-start | bytes 2359304 | tf_op jit(solution)/shard_map/ppermute | solution.py:64
  (99 other events, 1205.4 us)
Sparse Core Ops, SparseCore 0:
  13.7 48.6 all-gather.4
  69.4 28.4 all-gather.6
  123.5 107.1 all-gather.8
  256.9 59.5 all-gather.10
  363.2 54.9 reduce-scatter.10
  507.8 24.5 reduce-scatter.6
  535.4 100.9 reduce-scatter.8
  639.3 35.8 reduce-scatter.4
where the time goes:
time: 835 us; the launch traced here: 825 us
  waiting for transfers between devices  261 us (31%)
  other arithmetic  209 us (25%)
  matrix products  155 us (19%)
  local copies, waits for them, and re-layouts  83.1 us (10%)
  blocking collectives  51.3 us (6%)
  starting transfers between devices  49.7 us (6%)
  between operations  16.2 us (2%)
    dot_general x12, matrix products, dot(): lax.dot_general(a, b, (((ca,), (cb,)), ((), ())), preferred_element_type=...  111 us
    ppermute x20, waiting for transfers between devices, far(): return lax.ppermute(v, 'ctx', [(i, i ^ 2) for i in range(4)])  105 us
    ppermute x18, waiting for transfers between devices, side(): return lax.ppermute(v, 'tp', [(0, 1), (1, 0)])  88.6 us
    concatenate x4, other arithmetic, spread(): mine = jnp.concatenate([left_all, right_all], axis=1)  79 us
    psum x1, blocking collectives, body(): lax.psum(jnp.stack([jnp.sum(d_n1 * hat_one, axis=0), jnp.sum(d_n2 * hat_t...  51.3 us
    unnamed x208, local copies, waits for them, and re-layouts  27.8 us
    reduce_scatter x1, waiting for transfers between devices, body(): lax.psum_scatter(grad_qkv, 'fsdp', scatter_dimension=1, tiled=True)  25 us
    ppermute x20, starting transfers between devices, far(): return lax.ppermute(v, 'ctx', [(i, i ^ 2) for i in range(4)])  24.6 us
  transfers between devices with their start and end apart: 60, of which 28 were waited for; matrix products, arithmetic and copies ran while one was open for 44% of the time, Pallas kernels for 0%

commit v1 on v0

--- a/solution.py
+++ b/solution.py
@@ -251,8 +251,11 @@
     hat_one = x_own * inv_one
     input_grad = both_sides((d_mid + norm_back(d_n1, hat_one, inv_one, gain_one)).astype(BF16), t)
     gain_grads = lax.psum(
-        jnp.stack([jnp.sum(d_n1 * hat_one, axis=0), jnp.sum(d_n2 * hat_two, axis=0)]),
-        ("fsdp", "ctx", "tp"),
+        lax.psum(
+            jnp.stack([jnp.sum(d_n1 * hat_one, axis=0), jnp.sum(d_n2 * hat_two, axis=0)]),
+            ("ctx", "tp"),
+        ),
+        "fsdp",
     )
     shard_width = gain_attn.shape[0]
     gain_grads = lax.dynamic_slice_in_dim(

time: 835 us -> 839 us (level)
    psum x0 -> x1, blocking collectives: none -> 18.2 us  [body(): lax.psum(lax.psum(jnp.stack([jnp.sum(d_n1 * hat_one, axis=0), jnp.sum(d_n...]
    psum x1, blocking collectives: 51.3 us -> 36.5 us  [body(): lax.psum(jnp.stack([jnp.sum(d_n1 * hat_one, axis=0), jnp.sum(d_n2 * hat_t...]
where the time goes in v1:
time: 839 us; the launch traced here: 829 us
  waiting for transfers between devices  261 us (31%)
  other arithmetic  209 us (25%)
  matrix products  155 us (18%)
  local copies, waits for them, and re-layouts  83.1 us (10%)
  blocking collectives  54.7 us (7%)
  starting transfers between devices  49.7 us (6%)
  between operations  16.2 us (2%)
    dot_general x12, matrix products, dot(): lax.dot_general(a, b, (((ca,), (cb,)), ((), ())), preferred_element_type=...  111 us
    ppermute x20, waiting for transfers between devices, far(): return lax.ppermute(v, 'ctx', [(i, i ^ 2) for i in range(4)])  105 us
    ppermute x18, waiting for transfers between devices, side(): return lax.ppermute(v, 'tp', [(0, 1), (1, 0)])  88.6 us
    concatenate x4, other arithmetic, spread(): mine = jnp.concatenate([left_all, right_all], axis=1)  79 us
    psum x1, blocking collectives, body(): lax.psum(jnp.stack([jnp.sum(d_n1 * hat_one, axis=0), jnp.sum(d_n2 * hat_t...  36.5 us
    unnamed x208, local copies, waits for them, and re-layouts  27.9 us
    reduce_scatter x1, waiting for transfers between devices, body(): lax.psum_scatter(grad_qkv, 'fsdp', scatter_dimension=1, tiled=True)  25 us
    ppermute x20, starting transfers between devices, far(): return lax.ppermute(v, 'ctx', [(i, i ^ 2) for i in range(4)])  24.7 us
  transfers between devices with their start and end apart: 60, of which 28 were waited for; matrix products, arithmetic and copies ran while one was open for 44% of the time, Pallas kernels for 0%

profile of v1, /device:TPU:0, one launch (start us, length us, event | category | flops | bytes accessed | tf_op | source)
XLA Modules:
  0.0 828.8 jit_solution(9771869537621604506)
XLA Ops:
  15.6 3.0 collective-permute-start
  20.2 7.6 collective-permute-done
  31.3 15.3 %collective-permute-done.1 = bf16[384,1024]{1,0:T(8,128)(2,1)S(1)} collective-permute-done((bf16[384,1024]{1,0:T(8,128)(2,1)S(1)}, bf16[384,1024]{1,0:T(8,128)(2,1)S(1)}, u32[]{:S(2)}, u32[]{:S(2)}) %collective-permute-start.1) | collective-permute-done | bytes 786464 | tf_op jit(solution)/shard_map/ppermute | solution.py:64
  47.9 19.6 %maximum_maximum_fusion = bf16[768,2048]{1,0:T(8,128)(2,1)} fusion(bf16[384,1024]{1,0:T(8,128)(2,1)S(1)} %collective-permute-done.3, bf16[192,1024]{1,0:T(8,128)(2,1)S(1)} %collective-permute-done.2, bf16[192,1024]{1,0:T(8,128)(2,1)S(1)} %get-tuple-element.104, bf16[192,1024]{1,0:T(8,128)(2,1)S(1)} %get-tuple-element.102, ...), kind=kLoop, calls=%fused_computation.45 | loop fusion | flops 22020096 | bytes 6291456 | tf_op jit(solution)/shard_map/concatenate | solution.py:76
  69.9 5.4 or_and_fusion
  77.2 6.0 fusion.7
  83.3 3.0 fusion.26
  90.5 5.6 fusion.5
  96.1 6.0 fusion.6
  103.2 8.3 fusion.16
  111.5 3.3 convolution_convert_fusion
  125.5 4.2 add_convert_fusion.3
  132.2 17.4 %collective-permute-done.7 = bf16[384,1024]{1,0:T(8,128)(2,1)S(1)} collective-permute-done((bf16[384,1024]{1,0:T(8,128)(2,1)S(1)}, bf16[384,1024]{1,0:T(8,128)(2,1)S(1)}, u32[]{:S(2)}, u32[]{:S(2)}) %collective-permute-start.7) | collective-permute-done | bytes 786464 | tf_op jit(solution)/shard_map/ppermute | solution.py:56
  152.6 7.9 collective-permute-done.8
  165.9 6.9 collective-permute-done.22
  178.0 15.4 %collective-permute-done.23 = bf16[384,1024]{1,0:T(8,128)(2,1)S(1)} collective-permute-done((bf16[384,1024]{1,0:T(8,128)(2,1)S(1)}, bf16[384,1024]{1,0:T(8,128)(2,1)S(1)}, u32[]{:S(2)}, u32[]{:S(2)}) %collective-permute-start.23) | collective-permute-done | bytes 786464 | tf_op jit(solution)/shard_map/ppermute | solution.py:64
  195.3 19.8 %maximum_maximum_fusion.2 = bf16[768,2048]{1,0:T(8,128)(2,1)} fusion(bf16[384,1024]{1,0:T(8,128)(2,1)S(1)} %collective-permute-done.25, bf16[192,1024]{1,0:T(8,128)(2,1)S(1)} %collective-permute-done.24, bf16[192,1024]{1,0:T(8,128)(2,1)S(1)} %get-tuple-element.96, bf16[192,1024]{1,0:T(8,128)(2,1)S(1)} %get-tuple-element.94, ...), kind=kLoop, calls=%fused_computation.47 | loop fusion | flops 22020096 | bytes 6291456 | tf_op jit(solution)/shard_map/concatenate | solution.py:76
  217.2 18.0 %collective-permute-done.12 = bf16[384,1024]{1,0:T(8,128)(2,1)S(1)} collective-permute-done((bf16[384,1024]{1,0:T(8,128)(2,1)S(1)}, bf16[384,1024]{1,0:T(8,128)(2,1)S(1)}, u32[]{:S(2)}, u32[]{:S(2)}) %collective-permute-start.12) | collective-permute-done | bytes 786464 | tf_op jit(solution)/shard_map/ppermute | solution.py:64
  235.8 20.0 %maximum_maximum_fusion.1 = bf16[768,2048]{1,0:T(8,128)(2,1)} fusion(bf16[384,1024]{1,0:T(8,128)(2,1)S(1)} %collective-permute-done.14, bf16[192,1024]{1,0:T(8,128)(2,1)S(1)} %collective-permute-done.13, bf16[192,1024]{1,0:T(8,128)(2,1)S(1)} %get-tuple-element.100, bf16[192,1024]{1,0:T(8,128)(2,1)S(1)} %get-tuple-element.98, ...), kind=kLoop, calls=%fused_computation.46 | loop fusion | flops 22020096 | bytes 6291456 | tf_op jit(solution)/shard_map/concatenate | solution.py:76
  256.9 7.3 pad_maximum_fusion.2
  264.3 35.0 %fusion.121 = f32[1408,1536]{1,0:T(8,128)} fusion(bf16[1408,2048]{0,1:T(8,128)(2,1)} %all-gather.9.cloned.1.call-done, bf16[768,2048]{1,0:T(8,128)(2,1)} %collective-permute-done.15, bf16[384,1024]{1,0:T(8,128)(2,1)} %copy-done.73, bf16[192,1024]{1,0:T(8,128)(2,1)S(1)} %copy-done.61, bf16[192,1024]{1,0:T(8,128)(2,1)S(1)} %copy-done.42, ...), kind=kOutput, calls=%fused_computation.277 | convolution fusion | flops 8908701696 | bytes 20709376 | tf_op jit(solution)/shard_map/dot_general | solution.py:15
  299.4 17.1 %all-gather.11.cloned.1.call-done = bf16[704,2048]{1,0:T(8,128)(2,1)} async-done(((bf16[704,512]{1,0:T(8,128)(2,1)}), bf16[704,2048]{1,0:T(8,128)(2,1)}) %all-gather.11.cloned.1.call-update) | async-done | bytes 2883600 | tf_op jit(solution)/shard_map/all_gather | solution.py:169
  316.5 13.8 %multiply_convert_fusion.1 = (bf16[704,1536]{1,0:T(8,128)(2,1)S(1)}, bf16[704,1536]{1,0:T(8,128)(2,1)}, bf16[704,1536]{1,0:T(8,128)(2,1)S(1)}) fusion(f32[1408,1536]{1,0:T(8,128)} %fusion.121, bf16[704,2048]{1,0:T(8,128)(2,1)} %all-gather.11.cloned.1.call-done, bf16[1536,2048]{1,0:T(8,128)(2,1)} %pad_maximum_fusion.2), kind=kOutput, calls=%fused_computation.40 | convolution fusion | flops 4445405184 | bytes 24313856 | tf_op jit(solution)/shard_map/dot_general | solution.py:15
  330.3 12.3 %convolution_convert_fusion.3 = bf16[1536,2048]{1,0:T(8,128)(2,1)S(1)} fusion(bf16[1408,2048]{0,1:T(8,128)(2,1)S(1)} %copy-done.93, bf16[704,1536]{1,0:T(8,128)(2,1)} %get-tuple-element.48, bf16[704,1536]{1,0:T(8,128)(2,1)S(1)} %get-tuple-element.47), kind=kOutput, calls=%fused_computation.26 | convolution fusion | flops 8870166528 | bytes 16384000 | tf_op jit(solution)/shard_map/dot_general | solution.py:15
  347.2 5.3 convolution_convert_fusion.4
  356.6 6.4 convolution_convert_fusion.5
  363.2 4.2 add_convert_fusion.1
  370.8 4.2 add_convert_fusion.2
  376.5 11.5 %collective-permute-done.28 = bf16[384,1024]{1,0:T(8,128)(2,1)S(1)} collective-permute-done((bf16[384,1024]{1,0:T(8,128)(2,1)S(1)}, bf16[384,1024]{1,0:T(8,128)(2,1)S(1)}, u32[]{:S(2)}, u32[]{:S(2)}) %collective-permute-start.28) | collective-permute-done | bytes 786464 | tf_op jit(solution)/shard_map/ppermute | solution.py:56
  391.8 13.0 %collective-permute-done.17 = bf16[384,1024]{1,0:T(8,128)(2,1)S(1)} collective-permute-done((bf16[384,1024]{1,0:T(8,128)(2,1)S(1)}, bf16[384,1024]{1,0:T(8,128)(2,1)S(1)}, u32[]{:S(2)}, u32[]{:S(2)}) %collective-permute-start.17) | collective-permute-done | bytes 786464 | tf_op jit(solution)/shard_map/ppermute | solution.py:56
  408.7 6.3 collective-permute-done.29
  417.6 4.6 collective-permute-done.18
  428.4 7.9 collective-permute-done.32
  438.6 15.2 %collective-permute-done.33 = bf16[384,1024]{1,0:T(8,128)(2,1)S(1)} collective-permute-done((bf16[384,1024]{1,0:T(8,128)(2,1)S(1)}, bf16[384,1024]{1,0:T(8,128)(2,1)S(1)}, u32[]{:S(2)}, u32[]{:S(2)}) %collective-permute-start.33) | collective-permute-done | bytes 786464 | tf_op jit(solution)/shard_map/ppermute | solution.py:64
  455.1 19.7 %maximum_maximum_fusion.3 = bf16[768,2048]{1,0:T(8,128)(2,1)} fusion(bf16[384,1024]{1,0:T(8,128)(2,1)S(1)} %collective-permute-done.35, bf16[192,1024]{1,0:T(8,128)(2,1)S(1)} %collective-permute-done.34, bf16[192,1024]{1,0:T(8,128)(2,1)S(1)} %get-tuple-element.92, bf16[192,1024]{1,0:T(8,128)(2,1)S(1)} %get-tuple-element.90, ...), kind=kLoop, calls=%fused_computation.48 | loop fusion | flops 22020096 | bytes 6291456 | tf_op jit(solution)/shard_map/concatenate | solution.py:76
  476.6 17.1 %collective-permute-done.50 = bf16[704,512]{1,0:T(8,128)(2,1)} collective-permute-done((bf16[704,512]{1,0:T(8,128)(2,1)}, bf16[704,512]{1,0:T(8,128)(2,1)}, u32[]{:S(2)}, u32[]{:S(2)}) %collective-permute-start.50) | collective-permute-done | bytes 720928 | tf_op jit(solution)/shard_map/ppermute | solution.py:56
  496.3 5.9 pad_maximum_fusion.3
  502.2 2.7 copy-done.19
  504.9 2.8 convolution_convert_fusion.7
  507.8 16.6 %convolution_convert_fusion.1 = bf16[1408,2048]{1,0:T(8,128)(2,1)} fusion(bf16[704,1536]{1,0:T(8,128)(2,1)} %get-tuple-element.48, bf16[704,1536]{1,0:T(8,128)(2,1)} %copy-done.96, bf16[768,2048]{1,0:T(8,128)(2,1)} %collective-permute-done.15, bf16[384,1024]{1,0:T(8,128)(2,1)} %copy-done.73, bf16[192,1024]{1,0:T(8,128)(2,1)S(1)} %copy-done.62, ...), kind=kOutput, calls=%fused_computation.24 | convolution fusion | flops 8920236032 | bytes 16384000 | tf_op jit(solution)/shard_map/dot_general | solution.py:15
  527.8 3.4 maximum_select_fusion
  542.5 13.2 %fusion = (f32[2,1536]{1,0:T(2,128)S(1)}, f32[1536,1536,2]{1,0,2:T(8,128)}) fusion(f32[1536,1536,2]{1,0,2:T(8,128)} %copy-done.2, f32[2,1536]{1,0:T(2,128)S(1)} %log_add_fusion, pred[1536,1536]{0,1:T(8,128)(4,1)S(1)} %copy-done.3, bf16[1536,2,128]{0,2,1:T(8,128)(2,1)S(1)} %bitcast.232, bf16[1536,128]{0,1:T(8,128)(2,1)S(1)} %copy-done.12, ...), kind=kOutput, calls=%fused_computation.2 | convolution fusion | flops 1227813888 | bytes 41705472 | tf_op jit(solution)/shard_map/qhd,kd->hqk/dot_general | solution.py:236
  555.7 13.7 %fusion.2 = bf16[2,1536,1536]{1,2,0:T(8,128)(2,1)S(1)} fusion(f32[1536,1536,2]{1,0,2:T(8,128)} %get-tuple-element.125, f32[1536,1536,2]{1,0,2:T(8,128)} %copy-done.2, f32[2,1536]{1,0:T(2,128)S(1)} %get-tuple-element.124, f32[2,1536]{1,0:T(2,128)S(1)} %log_add_fusion, pred[1536,1536]{0,1:T(8,128)(4,1)S(1)} %copy-done.3), kind=kLoop, calls=%fused_computation.4 | loop fusion | flops 23592960 | bytes 49569792 | tf_op jit(solution)/shard_map/convert_element_type | solution.py:238
  569.4 4.0 convolution_bitcast_fusion
  573.4 12.0 %select_convert_fusion = (bf16[1536,128]{0,1:T(8,128)(2,1)}, f32[1536,128]{0,1:T(8,128)}) fusion(f32[1536,128]{0,1:T(8,128)} %convolution_bitcast_fusion, pred[]{:T(512)S(6)} %eq.48, bf16[1536,2,128]{0,2,1:T(8,128)(2,1)} %bitcast.233, f32[1536,1536,2]{1,0,2:T(8,128)} %copy-done.2, f32[2,1536]{1,0:T(2,128)S(1)} %log_add_fusion, ...), kind=kOutput, calls=%fused_computation.147 | convolution fusion | flops 1222311936 | bytes 23998464 | tf_op jit(solution)/shard_map/hqk,qhd->kd/dot_general | solution.py:241
  591.7 3.8 convolution_convert_fusion.2
  600.0 6.7 convolution_convert_fusion.6
  608.1 5.2 bitcast_convert_fusion
  613.4 22.9 %reduce-scatter.9.cloned.1.call-done = bf16[1408,512]{1,0:T(8,128)(2,1)} async-done(((bf16[1408,2048]{1,0:T(8,128)(2,1)}), bf16[1408,512]{1,0:T(8,128)(2,1)}) %reduce-scatter.9.cloned.1.call-update) | async-done | bytes 1441808 | tf_op jit(solution)/shard_map/reduce_scatter | solution.py:225
  639.6 3.4 broadcast_in_dim.90
  644.3 3.4 add_convert_fusion
  650.2 25.0 %reduce-scatter.5.cloned.1.call-done = bf16[384,512]{1,0:T(8,128)(2,1)} async-done(((bf16[384,2048]{1,0:T(8,128)(2,1)}), bf16[384,512]{1,0:T(8,128)(2,1)}) %reduce-scatter.5.cloned.1.call-update) | async-done | bytes 393232 | tf_op jit(solution)/shard_map/reduce_scatter | solution.py:248
  678.5 16.7 %collective-permute-done.44 = bf16[384,512]{1,0:T(8,128)(2,1)S(1)} collective-permute-done((bf16[384,512]{1,0:T(8,128)(2,1)}, bf16[384,512]{1,0:T(8,128)(2,1)S(1)}, u32[]{:S(2)}, u32[]{:S(2)}) %collective-permute-start.44) | collective-permute-done | bytes 393248 | tf_op jit(solution)/shard_map/ppermute | solution.py:56
  696.4 3.8 pad_maximum_fusion.5
  708.4 5.1 collective-permute-done.40
  718.9 36.5 %psum.14 = f32[2,2048]{1,0:T(2,128)S(1)} all-reduce(f32[2,2048]{1,0:T(2,128)S(1)} %pad_maximum_fusion.26), channel_id=1, replica_groups=mesh['fsdp'=4,'ctx'=4,'tp'=2] {'ctx','tp'}, use_global_device_ids=true, to_apply=%region_15.16 | all-reduce | flops 4096 | bytes 32768 | tf_op jit(solution)/shard_map/psum | solution.py:254
  755.4 18.2 %psum.15 = f32[2,2048]{1,0:T(2,128)S(1)} all-reduce(f32[2,2048]{1,0:T(2,128)S(1)} %psum.14), channel_id=1, replica_groups=mesh['fsdp'=4,'ctx'=4,'tp'=2] {'fsdp'}, use_global_device_ids=true, to_apply=%region_16.17 | all-reduce | flops 4096 | bytes 32768 | tf_op jit(solution)/shard_map/psum | solution.py:253
  774.3 4.5 fusion.32
  787.5 3.2 maximum_select_fusion.1
  795.8 4.7 fusion.123
  800.5 3.5 convert_bitcast_fusion
  804.0 6.2 copy.72
  810.3 5.2 convert_bitcast_fusion.1
  815.5 6.2 copy.71
  (458 shorter events, 160.6 us)
Async XLA Ops:
  7.2 248.7 %copy-start = (bf16[2816,512]{1,0:T(8,128)(2,1)S(1)}, bf16[2816,512]{1,0:T(8,128)(2,1)}, u32[]{:S(2)}) copy-start(bf16[2816,512]{1,0:T(8,128)(2,1)} %param.26) | copy-start | bytes 8650756
  7.2 68.2 %all-gather.5.cloned.1.call-start = ((), (), s32[]{:S(2)}) async-start(), calls=%async_computation.4 | async-start | bytes 2621440 | tf_op jit(solution)/shard_map/all_gather | solution.py:156
  13.6 97.9 %all-gather.7.cloned.1.call-start = ((), (), s32[]{:S(2)}) async-start(), calls=%async_computation.5 | async-start | bytes 1310720 | tf_op jit(solution)/shard_map/all_gather | solution.py:163
  15.6 12.1 %collective-permute-start = (bf16[192,1024]{1,0:T(8,128)(2,1)S(1)}, bf16[192,1024]{1,0:T(8,128)(2,1)S(1)}, u32[]{:S(2)}, u32[]{:S(2)}) collective-permute-start(bf16[192,1024]{1,0:T(8,128)(2,1)S(1)} %get-tuple-element.103), channel_id=1, source_target_pairs={{0,4},{2,6},{4,0},{6,2},{1,5},{3,7},{5,1},{7,3},{8,12},{10,14},{12... | collective-permute-start | bytes 1179656 | tf_op jit(solution)/shard_map/ppermute | solution.py:56
  18.6 11.0 %collective-permute-start.2 = (bf16[192,1024]{1,0:T(8,128)(2,1)S(1)}, bf16[192,1024]{1,0:T(8,128)(2,1)S(1)}, u32[]{:S(2)}, u32[]{:S(2)}) collective-permute-start(bf16[192,1024]{1,0:T(8,128)(2,1)S(1)} %get-tuple-element.104), channel_id=1, source_target_pairs={{0,1},{1,0},{2,3},{3,2},{4,5},{5,4},{6,7},{7,6},{8,9},{9,8},{10,11... | collective-permute-start | bytes 1179656 | tf_op jit(solution)/shard_map/ppermute | solution.py:64
  27.8 18.8 %collective-permute-start.1 = (bf16[384,1024]{1,0:T(8,128)(2,1)S(1)}, bf16[384,1024]{1,0:T(8,128)(2,1)S(1)}, u32[]{:S(2)}, u32[]{:S(2)}) collective-permute-start(bf16[384,1024]{1,0:T(8,128)(2,1)S(1)} %pad_maximum_fusion.13), channel_id=1, source_target_pairs={{0,1},{1,0},{2,3},{3,2},{4,5},{5,4},{6,7},{7,6},{8,9},{9,8},{10,11... | collective-permute-start | bytes 2359304 | tf_op jit(solution)/shard_map/ppermute | solution.py:64
  29.7 18.2 %collective-permute-start.3 = (bf16[384,1024]{1,0:T(8,128)(2,1)S(1)}, bf16[384,1024]{1,0:T(8,128)(2,1)S(1)}, u32[]{:S(2)}, u32[]{:S(2)}) collective-permute-start(bf16[384,1024]{1,0:T(8,128)(2,1)S(1)} %pad_maximum_fusion.14), channel_id=1, source_target_pairs={{0,4},{2,6},{4,0},{6,2},{1,5},{3,7},{5,1},{7,3},{8,12},{10,14},{12... | collective-permute-start | bytes 2359304 | tf_op jit(solution)/shard_map/ppermute | solution.py:56
  67.5 9.7 %collective-permute-start.4 = (bf16[768,2048]{1,0:T(8,128)(2,1)}, bf16[768,2048]{1,0:T(8,128)(2,1)}, u32[]{:S(2)}, u32[]{:S(2)}) collective-permute-start(bf16[768,2048]{1,0:T(8,128)(2,1)} %maximum_maximum_fusion), channel_id=1, source_target_pairs={{0,2},{2,0},{4,6},{6,4},{1,3},{3,1},{5,7},{7,5},{8,10},{10,8},{12,... | collective-permute-start | bytes 9437192 | tf_op jit(solution)/shard_map/ppermute | solution.py:60
  69.3 195.0 %all-gather.9.cloned.1.call-start = ((), (), s32[]{:S(2)}) async-start(), calls=%async_computation.6 | async-start | bytes 7208960 | tf_op jit(solution)/shard_map/all_gather | solution.py:168
  88.0 2.4 collective-permute-start.5
  119.5 6.0 collective-permute-start.6
  123.4 193.2 %all-gather.11.cloned.1.call-start = ((), (), s32[]{:S(2)}) async-start(), calls=%async_computation.7 | async-start | bytes 3604480 | tf_op jit(solution)/shard_map/all_gather | solution.py:169
  130.0 19.6 %collective-permute-start.7 = (bf16[384,1024]{1,0:T(8,128)(2,1)S(1)}, bf16[384,1024]{1,0:T(8,128)(2,1)S(1)}, u32[]{:S(2)}, u32[]{:S(2)}) collective-permute-start(bf16[384,1024]{1,0:T(8,128)(2,1)S(1)} %slice.429), channel_id=1, source_target_pairs={{0,4},{2,6},{4,0},{6,2},{1,5},{3,7},{5,1},{7,3},{8,12},{10,14},{12... | collective-permute-start | bytes 2359304 | tf_op jit(solution)/shard_map/ppermute | solution.py:56
  131.7 19.5 %collective-permute-start.9 = (bf16[384,1024]{1,0:T(8,128)(2,1)S(1)}, bf16[384,1024]{1,0:T(8,128)(2,1)S(1)}, u32[]{:S(2)}, u32[]{:S(2)}) collective-permute-start(bf16[384,1024]{1,0:T(8,128)(2,1)S(1)} %bitcast.231), channel_id=1, source_target_pairs={{0,1},{1,0},{2,3},{3,2},{4,5},{5,4},{6,7},{7,6},{8,9},{9,8},{10,11... | collective-permute-start | bytes 2359304 | tf_op jit(solution)/shard_map/ppermute | solution.py:64
  150.0 10.5 %collective-permute-start.8 = (bf16[192,1024]{1,0:T(8,128)(2,1)S(1)}, bf16[192,1024]{1,0:T(8,128)(2,1)S(1)}, u32[]{:S(2)}, u32[]{:S(2)}) collective-permute-start(bf16[192,1024]{1,0:T(8,128)(2,1)S(1)} %slice.431), channel_id=1, source_target_pairs={{0,1},{1,0},{2,3},{3,2},{4,5},{5,4},{6,7},{7,6},{8,9},{9,8},{10,11... | collective-permute-start | bytes 1179656 | tf_op jit(solution)/shard_map/ppermute | solution.py:64
  151.5 10.2 %collective-permute-start.10 = (bf16[192,1024]{1,0:T(8,128)(2,1)S(1)}, bf16[192,1024]{1,0:T(8,128)(2,1)S(1)}, u32[]{:S(2)}, u32[]{:S(2)}) collective-permute-start(bf16[192,1024]{1,0:T(8,128)(2,1)S(1)} %slice.436), channel_id=1, source_target_pairs={{0,4},{2,6},{4,0},{6,2},{1,5},{3,7},{5,1},{7,3},{8,12},{10,14},{12... | collective-permute-start | bytes 1179656 | tf_op jit(solution)/shard_map/ppermute | solution.py:56
  163.4 9.4 %collective-permute-start.22 = (bf16[192,1024]{1,0:T(8,128)(2,1)S(1)}, bf16[192,1024]{1,0:T(8,128)(2,1)S(1)}, u32[]{:S(2)}, u32[]{:S(2)}) collective-permute-start(bf16[192,1024]{1,0:T(8,128)(2,1)S(1)} %get-tuple-element.95), channel_id=1, source_target_pairs={{0,4},{2,6},{4,0},{6,2},{1,5},{3,7},{5,1},{7,3},{8,12},{10,14},{12... | collective-permute-start | bytes 1179656 | tf_op jit(solution)/shard_map/ppermute | solution.py:56
  164.7 10.3 %collective-permute-start.24 = (bf16[192,1024]{1,0:T(8,128)(2,1)S(1)}, bf16[192,1024]{1,0:T(8,128)(2,1)S(1)}, u32[]{:S(2)}, u32[]{:S(2)}) collective-permute-start(bf16[192,1024]{1,0:T(8,128)(2,1)S(1)} %get-tuple-element.96), channel_id=1, source_target_pairs={{0,1},{1,0},{2,3},{3,2},{4,5},{5,4},{6,7},{7,6},{8,9},{9,8},{10,11... | collective-permute-start | bytes 1179656 | tf_op jit(solution)/shard_map/ppermute | solution.py:64
  172.8 20.5 %collective-permute-start.23 = (bf16[384,1024]{1,0:T(8,128)(2,1)S(1)}, bf16[384,1024]{1,0:T(8,128)(2,1)S(1)}, u32[]{:S(2)}, u32[]{:S(2)}) collective-permute-start(bf16[384,1024]{1,0:T(8,128)(2,1)S(1)} %pad_maximum_fusion.17), channel_id=1, source_target_pairs={{0,1},{1,0},{2,3},{3,2},{4,5},{5,4},{6,7},{7,6},{8,9},{9,8},{10,11... | collective-permute-start | bytes 2359304 | tf_op jit(solution)/shard_map/ppermute | solution.py:64
  175.0 20.3 %collective-permute-start.25 = (bf16[384,1024]{1,0:T(8,128)(2,1)S(1)}, bf16[384,1024]{1,0:T(8,128)(2,1)S(1)}, u32[]{:S(2)}, u32[]{:S(2)}) collective-permute-start(bf16[384,1024]{1,0:T(8,128)(2,1)S(1)} %pad_maximum_fusion.18), channel_id=1, source_target_pairs={{0,4},{2,6},{4,0},{6,2},{1,5},{3,7},{5,1},{7,3},{8,12},{10,14},{12... | collective-permute-start | bytes 2359304 | tf_op jit(solution)/shard_map/ppermute | solution.py:56
  175.7 60.0 %copy-start.39 = (bf16[192,1024]{1,0:T(8,128)(2,1)}, bf16[192,1024]{1,0:T(8,128)(2,1)S(1)}, u32[]{:S(2)}) copy-start(bf16[192,1024]{1,0:T(8,128)(2,1)S(1)} %get-tuple-element.99) | copy-start | bytes 1179652
  175.8 60.0 %copy-start.41 = (bf16[192,1024]{1,0:T(8,128)(2,1)}, bf16[192,1024]{1,0:T(8,128)(2,1)S(1)}, u32[]{:S(2)}) copy-start(bf16[192,1024]{1,0:T(8,128)(2,1)S(1)} %get-tuple-element.100) | copy-start | bytes 1179652
  175.8 39.4 %collective-permute-start.11 = (bf16[192,1024]{1,0:T(8,128)(2,1)S(1)}, bf16[192,1024]{1,0:T(8,128)(2,1)S(1)}, u32[]{:S(2)}, u32[]{:S(2)}) collective-permute-start(bf16[192,1024]{1,0:T(8,128)(2,1)S(1)} %get-tuple-element.99), channel_id=1, source_target_pairs={{0,4},{2,6},{4,0},{6,2},{1,5},{3,7},{5,1},{7,3},{8,12},{10,14},{12... | collective-permute-start | bytes 1179656 | tf_op jit(solution)/shard_map/ppermute | solution.py:56
  177.5 38.5 %collective-permute-start.13 = (bf16[192,1024]{1,0:T(8,128)(2,1)S(1)}, bf16[192,1024]{1,0:T(8,128)(2,1)S(1)}, u32[]{:S(2)}, u32[]{:S(2)}) collective-permute-start(bf16[192,1024]{1,0:T(8,128)(2,1)S(1)} %get-tuple-element.100), channel_id=1, source_target_pairs={{0,1},{1,0},{2,3},{3,2},{4,5},{5,4},{6,7},{7,6},{8,9},{9,8},{10,11... | collective-permute-start | bytes 1179656 | tf_op jit(solution)/shard_map/ppermute | solution.py:64
  215.1 41.8 %collective-permute-start.26 = (bf16[768,2048]{1,0:T(8,128)(2,1)}, bf16[768,2048]{1,0:T(8,128)(2,1)}, u32[]{:S(2)}, u32[]{:S(2)}) collective-permute-start(bf16[768,2048]{1,0:T(8,128)(2,1)} %maximum_maximum_fusion.2), channel_id=1, source_target_pairs={{0,2},{2,0},{4,6},{6,4},{1,3},{3,1},{5,7},{7,5},{8,10},{10,8},{12,... | collective-permute-start | bytes 9437192 | tf_op jit(solution)/shard_map/ppermute | solution.py:60
  215.2 20.0 %collective-permute-start.12 = (bf16[384,1024]{1,0:T(8,128)(2,1)S(1)}, bf16[384,1024]{1,0:T(8,128)(2,1)S(1)}, u32[]{:S(2)}, u32[]{:S(2)}) collective-permute-start(bf16[384,1024]{1,0:T(8,128)(2,1)S(1)} %pad_maximum_fusion.15), channel_id=1, source_target_pairs={{0,1},{1,0},{2,3},{3,2},{4,5},{5,4},{6,7},{7,6},{8,9},{9,8},{10,11... | collective-permute-start | bytes 2359304 | tf_op jit(solution)/shard_map/ppermute | solution.py:64
  216.1 19.7 %collective-permute-start.14 = (bf16[384,1024]{1,0:T(8,128)(2,1)S(1)}, bf16[384,1024]{1,0:T(8,128)(2,1)S(1)}, u32[]{:S(2)}, u32[]{:S(2)}) collective-permute-start(bf16[384,1024]{1,0:T(8,128)(2,1)S(1)} %pad_maximum_fusion.16), channel_id=1, source_target_pairs={{0,4},{2,6},{4,0},{6,2},{1,5},{3,7},{5,1},{7,3},{8,12},{10,14},{12... | collective-permute-start | bytes 2359304 | tf_op jit(solution)/shard_map/ppermute | solution.py:56
  255.8 8.5 %collective-permute-start.15 = (bf16[768,2048]{1,0:T(8,128)(2,1)}, bf16[768,2048]{1,0:T(8,128)(2,1)}, u32[]{:S(2)}, u32[]{:S(2)}) collective-permute-start(bf16[768,2048]{1,0:T(8,128)(2,1)} %maximum_maximum_fusion.1), channel_id=1, source_target_pairs={{0,2},{2,0},{4,6},{6,4},{1,3},{3,1},{5,7},{7,5},{8,10},{10,8},{12,... | collective-permute-start | bytes 9437192 | tf_op jit(solution)/shard_map/ppermute | solution.py:60
  256.9 218.0 %reduce-scatter.11.cloned.1.call-start = ((), (), s32[]{:S(2)}) async-start(), calls=%async_computation.11 | async-start | bytes 3604480 | tf_op jit(solution)/shard_map/reduce_scatter | solution.py:226
  347.2 16.0 %collective-permute-start.27 = (bf16[768,2048]{1,0:T(8,128)(2,1)}, bf16[768,2048]{1,0:T(8,128)(2,1)}, u32[]{:S(2)}, u32[]{:S(2)}) collective-permute-start(bf16[768,2048]{1,0:T(8,128)(2,1)} %slice.460), channel_id=1, source_target_pairs={{0,2},{2,0},{4,6},{6,4},{1,3},{3,1},{5,7},{7,5},{8,10},{10,8},{12,... | collective-permute-start | bytes 9437192 | tf_op jit(solution)/shard_map/ppermute | solution.py:60
  356.1 14.6 %collective-permute-start.16 = (bf16[768,2048]{1,0:T(8,128)(2,1)}, bf16[768,2048]{1,0:T(8,128)(2,1)}, u32[]{:S(2)}, u32[]{:S(2)}) collective-permute-start(bf16[768,2048]{1,0:T(8,128)(2,1)} %slice.445), channel_id=1, source_target_pairs={{0,2},{2,0},{4,6},{6,4},{1,3},{3,1},{5,7},{7,5},{8,10},{10,8},{12,... | collective-permute-start | bytes 9437192 | tf_op jit(solution)/shard_map/ppermute | solution.py:60
  363.1 235.9 %reduce-scatter.7.cloned.1.call-start = ((), (), s32[]{:S(2)}) async-start(), calls=%async_computation.9 | async-start | bytes 1310720 | tf_op jit(solution)/shard_map/reduce_scatter | solution.py:232
  367.6 20.5 %collective-permute-start.28 = (bf16[384,1024]{1,0:T(8,128)(2,1)S(1)}, bf16[384,1024]{1,0:T(8,128)(2,1)S(1)}, u32[]{:S(2)}, u32[]{:S(2)}) collective-permute-start(bf16[384,1024]{1,0:T(8,128)(2,1)S(1)} %slice.462), channel_id=1, source_target_pairs={{0,4},{2,6},{4,0},{6,2},{1,5},{3,7},{5,1},{7,3},{8,12},{10,14},{12... | collective-permute-start | bytes 2359304 | tf_op jit(solution)/shard_map/ppermute | solution.py:56
  369.2 20.7 %collective-permute-start.30 = (bf16[384,1024]{1,0:T(8,128)(2,1)S(1)}, bf16[384,1024]{1,0:T(8,128)(2,1)S(1)}, u32[]{:S(2)}, u32[]{:S(2)}) collective-permute-start(bf16[384,1024]{1,0:T(8,128)(2,1)S(1)} %bitcast.230), channel_id=1, source_target_pairs={{0,1},{1,0},{2,3},{3,2},{4,5},{5,4},{6,7},{7,6},{8,9},{9,8},{10,11... | collective-permute-start | bytes 2359304 | tf_op jit(solution)/shard_map/ppermute | solution.py:64
  375.1 29.7 %collective-permute-start.17 = (bf16[384,1024]{1,0:T(8,128)(2,1)S(1)}, bf16[384,1024]{1,0:T(8,128)(2,1)S(1)}, u32[]{:S(2)}, u32[]{:S(2)}) collective-permute-start(bf16[384,1024]{1,0:T(8,128)(2,1)S(1)} %slice.447), channel_id=1, source_target_pairs={{0,4},{2,6},{4,0},{6,2},{1,5},{3,7},{5,1},{7,3},{8,12},{10,14},{12... | collective-permute-start | bytes 2359304 | tf_op jit(solution)/shard_map/ppermute | solution.py:56
  375.9 30.9 %collective-permute-start.19 = (bf16[384,1024]{1,0:T(8,128)(2,1)S(1)}, bf16[384,1024]{1,0:T(8,128)(2,1)S(1)}, u32[]{:S(2)}, u32[]{:S(2)}) collective-permute-start(bf16[384,1024]{1,0:T(8,128)(2,1)S(1)} %bitcast.229), channel_id=1, source_target_pairs={{0,1},{1,0},{2,3},{3,2},{4,5},{5,4},{6,7},{7,6},{8,9},{9,8},{10,11... | collective-permute-start | bytes 2359304 | tf_op jit(solution)/shard_map/ppermute | solution.py:64
  388.4 26.6 %collective-permute-start.29 = (bf16[192,1024]{1,0:T(8,128)(2,1)S(1)}, bf16[192,1024]{1,0:T(8,128)(2,1)S(1)}, u32[]{:S(2)}, u32[]{:S(2)}) collective-permute-start(bf16[192,1024]{1,0:T(8,128)(2,1)S(1)} %slice.464), channel_id=1, source_target_pairs={{0,1},{1,0},{2,3},{3,2},{4,5},{5,4},{6,7},{7,6},{8,9},{9,8},{10,11... | collective-permute-start | bytes 1179656 | tf_op jit(solution)/shard_map/ppermute | solution.py:64
  390.3 25.8 %collective-permute-start.31 = (bf16[192,1024]{1,0:T(8,128)(2,1)S(1)}, bf16[192,1024]{1,0:T(8,128)(2,1)S(1)}, u32[]{:S(2)}, u32[]{:S(2)}) collective-permute-start(bf16[192,1024]{1,0:T(8,128)(2,1)S(1)} %slice.469), channel_id=1, source_target_pairs={{0,4},{2,6},{4,0},{6,2},{1,5},{3,7},{5,1},{7,3},{8,12},{10,14},{12... | collective-permute-start | bytes 1179656 | tf_op jit(solution)/shard_map/ppermute | solution.py:56
  405.2 17.0 %collective-permute-start.18 = (bf16[192,1024]{1,0:T(8,128)(2,1)S(1)}, bf16[192,1024]{1,0:T(8,128)(2,1)S(1)}, u32[]{:S(2)}, u32[]{:S(2)}) collective-permute-start(bf16[192,1024]{1,0:T(8,128)(2,1)S(1)} %slice.449), channel_id=1, source_target_pairs={{0,1},{1,0},{2,3},{3,2},{4,5},{5,4},{6,7},{7,6},{8,9},{9,8},{10,11... | collective-permute-start | bytes 1179656 | tf_op jit(solution)/shard_map/ppermute | solution.py:64
  407.2 16.1 %collective-permute-start.20 = (bf16[192,1024]{1,0:T(8,128)(2,1)S(1)}, bf16[192,1024]{1,0:T(8,128)(2,1)S(1)}, u32[]{:S(2)}, u32[]{:S(2)}) collective-permute-start(bf16[192,1024]{1,0:T(8,128)(2,1)S(1)} %slice.454), channel_id=1, source_target_pairs={{0,4},{2,6},{4,0},{6,2},{1,5},{3,7},{5,1},{7,3},{8,12},{10,14},{12... | collective-permute-start | bytes 1179656 | tf_op jit(solution)/shard_map/ppermute | solution.py:56
  426.3 10.0 %collective-permute-start.32 = (bf16[192,1024]{1,0:T(8,128)(2,1)S(1)}, bf16[192,1024]{1,0:T(8,128)(2,1)S(1)}, u32[]{:S(2)}, u32[]{:S(2)}) collective-permute-start(bf16[192,1024]{1,0:T(8,128)(2,1)S(1)} %get-tuple-element.91), channel_id=1, source_target_pairs={{0,4},{2,6},{4,0},{6,2},{1,5},{3,7},{5,1},{7,3},{8,12},{10,14},{12... | collective-permute-start | bytes 1179656 | tf_op jit(solution)/shard_map/ppermute | solution.py:56
  426.9 10.9 %collective-permute-start.34 = (bf16[192,1024]{1,0:T(8,128)(2,1)S(1)}, bf16[192,1024]{1,0:T(8,128)(2,1)S(1)}, u32[]{:S(2)}, u32[]{:S(2)}) collective-permute-start(bf16[192,1024]{1,0:T(8,128)(2,1)S(1)} %get-tuple-element.92), channel_id=1, source_target_pairs={{0,1},{1,0},{2,3},{3,2},{4,5},{5,4},{6,7},{7,6},{8,9},{9,8},{10,11... | collective-permute-start | bytes 1179656 | tf_op jit(solution)/shard_map/ppermute | solution.py:64
  436.3 17.5 %collective-permute-start.33 = (bf16[384,1024]{1,0:T(8,128)(2,1)S(1)}, bf16[384,1024]{1,0:T(8,128)(2,1)S(1)}, u32[]{:S(2)}, u32[]{:S(2)}) collective-permute-start(bf16[384,1024]{1,0:T(8,128)(2,1)S(1)} %pad_maximum_fusion.19), channel_id=1, source_target_pairs={{0,1},{1,0},{2,3},{3,2},{4,5},{5,4},{6,7},{7,6},{8,9},{9,8},{10,11... | collective-permute-start | bytes 2359304 | tf_op jit(solution)/shard_map/ppermute | solution.py:64
  437.9 17.2 %collective-permute-start.35 = (bf16[384,1024]{1,0:T(8,128)(2,1)S(1)}, bf16[384,1024]{1,0:T(8,128)(2,1)S(1)}, u32[]{:S(2)}, u32[]{:S(2)}) collective-permute-start(bf16[384,1024]{1,0:T(8,128)(2,1)S(1)} %pad_maximum_fusion.20), channel_id=1, source_target_pairs={{0,4},{2,6},{4,0},{6,2},{1,5},{3,7},{5,1},{7,3},{8,12},{10,14},{12... | collective-permute-start | bytes 2359304 | tf_op jit(solution)/shard_map/ppermute | solution.py:56
  474.8 21.4 %collective-permute-start.36 = (bf16[768,2048]{1,0:T(8,128)(2,1)}, bf16[768,2048]{1,0:T(8,128)(2,1)}, u32[]{:S(2)}, u32[]{:S(2)}) collective-permute-start(bf16[768,2048]{1,0:T(8,128)(2,1)} %maximum_maximum_fusion.3), channel_id=1, source_target_pairs={{0,2},{2,0},{4,6},{6,4},{1,3},{3,1},{5,7},{7,5},{8,10},{10,8},{12,... | collective-permute-start | bytes 9437192 | tf_op jit(solution)/shard_map/ppermute | solution.py:60
  474.8 18.9 %collective-permute-start.50 = (bf16[704,512]{1,0:T(8,128)(2,1)}, bf16[704,512]{1,0:T(8,128)(2,1)}, u32[]{:S(2)}, u32[]{:S(2)}) collective-permute-start(bf16[704,512]{1,0:T(8,128)(2,1)} %reduce-scatter.11.cloned.1.call-done), channel_id=1, source_target_pairs={{0,4},{2,6},{4,0},{6,2},{1,5},{3,7},{5,1},{7,3},{8,12},{10,14},{12... | collective-permute-start | bytes 2162696 | tf_op jit(solution)/shard_map/ppermute | solution.py:56
  475.5 52.3 %collective-permute-start.21 = (bf16[192,2048]{1,0:T(8,128)(2,1)}, bf16[192,2048]{1,0:T(8,128)(2,1)}, u32[]{:S(2)}, u32[]{:S(2)}) collective-permute-start(bf16[192,2048]{1,0:T(8,128)(2,1)} %get-tuple-element.62), channel_id=1, source_target_pairs={{0,1},{1,0},{2,3},{3,2},{4,5},{5,4},{6,7},{7,6},{8,9},{9,8},{10,11... | collective-permute-start | bytes 2359304 | tf_op jit(solution)/shard_map/ppermute | solution.py:64
  496.2 39.9 %collective-permute-start.51 = (bf16[2,704,512]{2,1,0:T(8,128)(2,1)}, bf16[2,704,512]{2,1,0:T(8,128)(2,1)}, u32[]{:S(2)}, u32[]{:S(2)}) collective-permute-start(bf16[2,704,512]{2,1,0:T(8,128)(2,1)} %pad_maximum_fusion.11), channel_id=1, source_target_pairs={{0,2},{2,0},{4,6},{6,4},{1,3},{3,1},{5,7},{7,5},{8,10},{10,8},{12,... | collective-permute-start | bytes 4325384 | tf_op jit(solution)/shard_map/ppermute | solution.py:60
  507.7 128.7 %reduce-scatter.9.cloned.1.call-start = ((), (), s32[]{:S(2)}) async-start(), calls=%async_computation.10 | async-start | bytes 7208960 | tf_op jit(solution)/shard_map/reduce_scatter | solution.py:225
  524.4 150.8 %reduce-scatter.5.cloned.1.call-start = ((), (), s32[]{:S(2)}) async-start(), calls=%async_computation.8 | async-start | bytes 1966080 | tf_op jit(solution)/shard_map/reduce_scatter | solution.py:248
  585.5 4.1 collective-permute-start.37
  599.0 45.1 %collective-permute-start.38 = (bf16[768,2048]{1,0:T(8,128)(2,1)}, bf16[768,2048]{1,0:T(8,128)(2,1)}, u32[]{:S(2)}, u32[]{:S(2)}) collective-permute-start(bf16[768,2048]{1,0:T(8,128)(2,1)} %slice.483), channel_id=1, source_target_pairs={{0,2},{2,0},{4,6},{6,4},{1,3},{3,1},{5,7},{7,5},{8,10},{10,8},{12,... | collective-permute-start | bytes 9437192 | tf_op jit(solution)/shard_map/ppermute | solution.py:60
  599.1 8.9 %collective-permute-start.46 = (bf16[256,512]{1,0:T(8,128)(2,1)}, bf16[256,512]{1,0:T(8,128)(2,1)S(1)}, u32[]{:S(2)}, u32[]{:S(2)}) collective-permute-start(bf16[256,512]{1,0:T(8,128)(2,1)} %reduce-scatter.7.cloned.1.call-done), channel_id=1, source_target_pairs={{0,4},{2,6},{4,0},{6,2},{1,5},{3,7},{5,1},{7,3},{8,12},{10,14},{12... | collective-permute-start | bytes 786440 | tf_op jit(solution)/shard_map/ppermute | solution.py:56
  608.0 29.8 %collective-permute-start.47 = (bf16[2,256,512]{2,1,0:T(8,128)(2,1)S(1)}, bf16[2,256,512]{2,1,0:T(8,128)(2,1)S(1)}, u32[]{:S(2)}, u32[]{:S(2)}) collective-permute-start(bf16[2,256,512]{2,1,0:T(8,128)(2,1)S(1)} %pad_maximum_fusion.24), channel_id=1, source_target_pairs={{0,2},{2,0},{4,6},{6,4},{1,3},{3,1},{5,7},{7,5},{8,10},{10,8},{12,... | collective-permute-start | bytes 1572872 | tf_op jit(solution)/shard_map/ppermute | solution.py:60
  636.4 60.0 %collective-permute-start.48 = (bf16[1408,512]{1,0:T(8,128)(2,1)}, bf16[1408,512]{1,0:T(8,128)(2,1)}, u32[]{:S(2)}, u32[]{:S(2)}) collective-permute-start(bf16[1408,512]{1,0:T(8,128)(2,1)} %reduce-scatter.9.cloned.1.call-done), channel_id=1, source_target_pairs={{0,4},{2,6},{4,0},{6,2},{1,5},{3,7},{5,1},{7,3},{8,12},{10,14},{12... | collective-permute-start | bytes 4325384 | tf_op jit(solution)/shard_map/ppermute | solution.py:56
  649.8 50.9 %collective-permute-start.39 = (bf16[384,1024]{1,0:T(8,128)(2,1)}, bf16[384,1024]{1,0:T(8,128)(2,1)}, u32[]{:S(2)}, u32[]{:S(2)}) collective-permute-start(bf16[384,1024]{1,0:T(8,128)(2,1)} %slice.485), channel_id=1, source_target_pairs={{0,4},{2,6},{4,0},{6,2},{1,5},{3,7},{5,1},{7,3},{8,12},{10,14},{12... | collective-permute-start | bytes 2359304 | tf_op jit(solution)/shard_map/ppermute | solution.py:56
  675.2 20.1 %collective-permute-start.44 = (bf16[384,512]{1,0:T(8,128)(2,1)}, bf16[384,512]{1,0:T(8,128)(2,1)S(1)}, u32[]{:S(2)}, u32[]{:S(2)}) collective-permute-start(bf16[384,512]{1,0:T(8,128)(2,1)} %reduce-scatter.5.cloned.1.call-done), channel_id=1, source_target_pairs={{0,4},{2,6},{4,0},{6,2},{1,5},{3,7},{5,1},{7,3},{8,12},{10,14},{12... | collective-permute-start | bytes 1179656 | tf_op jit(solution)/shard_map/ppermute | solution.py:56
  676.8 27.1 %collective-permute-start.41 = (bf16[384,1024]{1,0:T(8,128)(2,1)S(1)}, bf16[384,1024]{1,0:T(8,128)(2,1)S(1)}, u32[]{:S(2)}, u32[]{:S(2)}) collective-permute-start(bf16[384,1024]{1,0:T(8,128)(2,1)S(1)} %bitcast.228), channel_id=1, source_target_pairs={{0,1},{1,0},{2,3},{3,2},{4,5},{5,4},{6,7},{7,6},{8,9},{9,8},{10,11... | collective-permute-start | bytes 2359304 | tf_op jit(solution)/shard_map/ppermute | solution.py:64
  696.3 82.4 %collective-permute-start.45 = (bf16[2,384,512]{2,1,0:T(8,128)(2,1)}, bf16[2,384,512]{2,1,0:T(8,128)(2,1)}, u32[]{:S(2)}, u32[]{:S(2)}) collective-permute-start(bf16[2,384,512]{2,1,0:T(8,128)(2,1)} %pad_maximum_fusion.21), channel_id=1, source_target_pairs={{0,2},{2,0},{4,6},{6,4},{1,3},{3,1},{5,7},{7,5},{8,10},{10,8},{12,... | collective-permute-start | bytes 2359304 | tf_op jit(solution)/shard_map/ppermute | solution.py:60
  700.2 90.5 %collective-permute-start.49 = (bf16[2,1408,512]{2,1,0:T(8,128)(2,1)}, bf16[2,1408,512]{2,1,0:T(8,128)(2,1)}, u32[]{:S(2)}, u32[]{:S(2)}) collective-permute-start(bf16[2,1408,512]{2,1,0:T(8,128)(2,1)} %pad_maximum_fusion.5), channel_id=1, source_target_pairs={{0,2},{2,0},{4,6},{6,4},{1,3},{3,1},{5,7},{7,5},{8,10},{10,8},{12,... | collective-permute-start | bytes 8650760 | tf_op jit(solution)/shard_map/ppermute | solution.py:60
  702.4 11.1 %collective-permute-start.40 = (bf16[192,1024]{1,0:T(8,128)(2,1)S(1)}, bf16[192,1024]{1,0:T(8,128)(2,1)S(1)}, u32[]{:S(2)}, u32[]{:S(2)}) collective-permute-start(bf16[192,1024]{1,0:T(8,128)(2,1)S(1)} %slice.487), channel_id=1, source_target_pairs={{0,1},{1,0},{2,3},{3,2},{4,5},{5,4},{6,7},{7,6},{8,9},{9,8},{10,11... | collective-permute-start | bytes 1179656 | tf_op jit(solution)/shard_map/ppermute | solution.py:64
  704.3 10.8 %collective-permute-start.42 = (bf16[192,1024]{1,0:T(8,128)(2,1)S(1)}, bf16[192,1024]{1,0:T(8,128)(2,1)S(1)}, u32[]{:S(2)}, u32[]{:S(2)}) collective-permute-start(bf16[192,1024]{1,0:T(8,128)(2,1)S(1)} %slice.492), channel_id=1, source_target_pairs={{0,4},{2,6},{4,0},{6,2},{1,5},{3,7},{5,1},{7,3},{8,12},{10,14},{12... | collective-permute-start | bytes 1179656 | tf_op jit(solution)/shard_map/ppermute | solution.py:56
  716.1 58.1 %copy-start.16 = (f32[1,192,1024]{2,1,0:T(8,128)S(1)}, f32[1,192,1024]{2,1,0:T(8,128)}, u32[]{:S(2)}) copy-start(f32[1,192,1024]{2,1,0:T(8,128)} %get-tuple-element.81) | copy-start | bytes 2359300
  718.1 69.3 %collective-permute-start.43 = (bf16[192,2048]{1,0:T(8,128)(2,1)}, bf16[192,2048]{1,0:T(8,128)(2,1)}, u32[]{:S(2)}, u32[]{:S(2)}) collective-permute-start(bf16[192,2048]{1,0:T(8,128)(2,1)} %fusion.38), channel_id=1, source_target_pairs={{0,1},{1,0},{2,3},{3,2},{4,5},{5,4},{6,7},{7,6},{8,9},{9,8},{10,11... | collective-permute-start | bytes 2359304 | tf_op jit(solution)/shard_map/ppermute | solution.py:64
  (99 other events, 1208.8 us)
Sparse Core Ops, SparseCore 0:
  13.7 48.6 all-gather.4
  69.4 28.4 all-gather.6
  123.5 107.1 all-gather.8
  256.9 59.5 all-gather.10
  363.2 54.9 reduce-scatter.10
  507.8 24.6 reduce-scatter.6
  535.4 100.9 reduce-scatter.8
  639.4 35.7 reduce-scatter.4
